TPU v7x, 128 devices: a whole 4x4x4 slice. The times are simulated.
128 devices in a mesh: seq: 16 (over z, y_lo, core), head: 8 (over x, y_hi).
Axes of the slice: x: 4, y: 4 (y_hi: 2, y_lo: 2; y = y_hi * 2 + y_lo), z: 4, core: 2. Of those that a mesh axis runs over, the one named last changes fastest.
Arguments:
- queries: bfloat16 [32768, 4096], P(('seq', 'head')), may hold values from -6 to 6
- key_rows: bfloat16 [32768, 2048], P(('seq', 'head')), may hold values from -6 to 6
- value_rows: bfloat16 [32768, 2048], P(('seq', 'head')), may hold values from -6 to 6
- output_grad: bfloat16 [32768, 4096], P(('seq', 'head')), may hold values from -6 to 6
Outputs:
- query_grad: bfloat16 [32768, 4096], P(('seq', 'head'))
- key_grad: bfloat16 [32768, 2048], P(('seq', 'head'))
- value_grad: bfloat16 [32768, 2048], P(('seq', 'head'))
All inputs are finite; a program needn't handle non-finite values.
Results may differ from a plain program's by a relative error of at most 0.012.
Values may be sent and summed in bfloat16 or wider, within the bound.
A program may use at most 256 MiB of HBM per device.

v0:
```python
import math

import jax
import jax.numpy as jnp
from jax import lax
from jax.sharding import PartitionSpec as P

HEAD_DIM = 128
WINDOW = 1024
GROUP = 2


score_scale = 168.0 ** (-0.5)


def shifted(value, axis, steps):
    count = lax.axis_size(axis)
    initial, last = (max(0, -steps), min(count, count - steps))
    return lax.ppermute(value, axis, [(source, source + steps) for source in range(initial, last)])


def band_mask(query_pos, key_pos):
    offset = query_pos[:, None] - key_pos[None, :]
    return (offset >= 0) & (offset < WINDOW) & (key_pos[None, :] >= 0)


def block_grads(query_block, key_block, value_block, grad_block, allowed):
    scores = (
        jnp.einsum("qhgd,khd->hgqk", query_block, key_block, preferred_element_type=jnp.float32)
        * score_scale
    )
    scores = jnp.where(allowed, scores, -jnp.inf)
    row_peak = jnp.max(scores, axis=-1, keepdims=True)
    raised = jnp.exp(scores - row_peak)
    probability = raised / jnp.sum(raised, axis=-1, keepdims=True)
    prob_grad = jnp.einsum(
        "qhgd,khd->hgqk", grad_block, value_block, preferred_element_type=jnp.float32
    )
    row_centre = jnp.sum(probability * prob_grad, axis=-1, keepdims=True)
    score_grad = (probability * (prob_grad - row_centre)).astype(jnp.bfloat16)
    prob_low = probability.astype(jnp.bfloat16)
    query_part = (
        jnp.einsum("hgqk,khd->qhgd", score_grad, key_block, preferred_element_type=jnp.float32)
        * score_scale
    )
    key_part = (
        jnp.einsum("hgqk,qhgd->khd", score_grad, query_block, preferred_element_type=jnp.float32)
        * score_scale
    )
    value_part = jnp.einsum(
        "hgqk,qhgd->khd", prob_low, grad_block, preferred_element_type=jnp.float32
    )
    return (query_part, key_part, value_part)


def band_grads(query_heads, key_ext, value_ext, grad_heads, first_pos):
    row_count = query_heads.shape[0]
    kv_count = key_ext.shape[1]
    block_rows = math.gcd(row_count, 512)
    head_block = math.gcd(kv_count, 4)
    key_acc = jnp.zeros(key_ext.shape, jnp.float32)
    value_acc = jnp.zeros(value_ext.shape, jnp.float32)
    query_rows = []
    for begin_row in range(0, row_count, block_rows):
        end_keys = begin_row + block_rows + WINDOW
        query_pos = first_pos + begin_row + jnp.arange(block_rows, dtype=jnp.int32)
        key_pos = first_pos + begin_row - WINDOW + jnp.arange(block_rows + WINDOW, dtype=jnp.int32)
        allowed = band_mask(query_pos, key_pos)
        query_part, key_part, value_part = block_grads(
            query_heads[begin_row : begin_row + block_rows, 0:head_block],
            key_ext[begin_row:end_keys, 0:head_block],
            value_ext[begin_row:end_keys, 0:head_block],
            grad_heads[begin_row : begin_row + block_rows, 0:head_block],
            allowed,
        )
        key_acc = key_acc.at[begin_row:end_keys, 0:head_block].add(key_part)
        value_acc = value_acc.at[begin_row:end_keys, 0:head_block].add(value_part)
        query_rows.append(query_part)
    return (jnp.concatenate(query_rows, axis=0), key_acc, value_acc)


def local(queries, key_rows, value_rows, output_grad):
    exchanged = (
        lax.all_to_all(queries, "head", split_axis=1, concat_axis=0, tiled=True),
        lax.all_to_all(key_rows, "head", split_axis=1, concat_axis=0, tiled=True),
        lax.all_to_all(value_rows, "head", split_axis=1, concat_axis=0, tiled=True),
        lax.all_to_all(output_grad, "head", split_axis=1, concat_axis=0, tiled=True),
    )
    query_local, key_local, value_local, grad_local = exchanged
    row_count = query_local.shape[0]
    kv_local = key_local.shape[1] // HEAD_DIM
    query_heads = query_local.reshape(row_count, kv_local, GROUP, HEAD_DIM)
    grad_heads = grad_local.reshape(row_count, kv_local, GROUP, HEAD_DIM)
    key_heads = key_local.reshape(row_count, kv_local, HEAD_DIM)
    value_heads = value_local.reshape(row_count, kv_local, HEAD_DIM)
    tail_rows = shifted(
        (key_heads[row_count - WINDOW :], value_heads[row_count - WINDOW :]), "seq", 1
    )
    key_ext = jnp.concatenate([tail_rows[0], key_heads], axis=0)
    value_ext = jnp.concatenate([tail_rows[1], value_heads], axis=0)
    first_pos = lax.axis_index("seq") * row_count
    query_part, key_part, value_part = band_grads(
        query_heads, key_ext, value_ext, grad_heads, first_pos
    )
    returned = (
        shifted(key_part[:WINDOW].astype(jnp.bfloat16), "seq", -1).astype(jnp.float32),
        shifted(value_part[:WINDOW].astype(jnp.bfloat16), "seq", -1).astype(jnp.float32),
    )
    key_total = key_part[WINDOW:].at[row_count - WINDOW :].add(returned[0])
    value_total = value_part[WINDOW:].at[row_count - WINDOW :].add(returned[1])
    outgoing = (
        query_part.astype(jnp.bfloat16).reshape(row_count, -1),
        key_total.astype(jnp.bfloat16).reshape(row_count, -1),
        value_total.astype(jnp.bfloat16).reshape(row_count, -1),
    )
    query_grad, key_grad, value_grad = (
        lax.all_to_all(outgoing[0], "head", split_axis=0, concat_axis=1, tiled=True),
        lax.all_to_all(outgoing[1], "head", split_axis=0, concat_axis=1, tiled=True),
        lax.all_to_all(outgoing[2], "head", split_axis=0, concat_axis=1, tiled=True),
    )
    return (query_grad, key_grad, value_grad)


def solution(mesh):
    placed = (
        P(("seq", "head"), None),
        P(("seq", "head"), None),
        P(("seq", "head"), None),
        P(("seq", "head"), None),
    )
    return jax.shard_map(
        local,
        mesh=mesh,
        in_specs=placed,
        out_specs=(P(("seq", "head"), None), P(("seq", "head"), None), P(("seq", "head"), None)),
        check_vma=False,
    )
```

profile of v0, /device:TPU:0, one launch (start us, length us, event | category | flops | bytes accessed | tf_op | source)
XLA Modules:
  0.0 376.7 jit_solution(1850466346074381908)
XLA Ops:
  0.6 2.3 copy.337
  2.9 7.0 %all-to-all-start = ((bf16[256,8,256]{2,0,1:T(8,128)(2,1)}), bf16[256,8,256]{2,0,1:T(8,128)(2,1)S(1)}, u32[]{:S(2)}, u32[]{:S(2)}) async-start(bf16[256,8,256]{2,0,1:T(8,128)(2,1)} %bitcast.287), calls=%async_computation | async-start | bytes 2097152 | tf_op jit(solution)/shard_map/all_to_all | solution.py:85
  9.9 2.3 copy.336
  12.2 13.6 %all-to-all-done = bf16[256,8,256]{2,0,1:T(8,128)(2,1)S(1)} async-done(((bf16[256,8,256]{2,0,1:T(8,128)(2,1)}), bf16[256,8,256]{2,0,1:T(8,128)(2,1)S(1)}, u32[]{:S(2)}, u32[]{:S(2)}) %all-to-all-start) | async-done | bytes 1048608 | tf_op jit(solution)/shard_map/all_to_all | solution.py:85
  25.8 4.1 %all-to-all-start.2 = ((bf16[256,8,256]{2,0,1:T(8,128)(2,1)}), bf16[256,8,256]{2,0,1:T(8,128)(2,1)S(1)}, u32[]{:S(2)}, u32[]{:S(2)}) async-start(bf16[256,8,256]{2,0,1:T(8,128)(2,1)} %bitcast.286), calls=%async_computation.2 | async-start | bytes 2097152 | tf_op jit(solution)/shard_map/all_to_all | solution.py:86
  29.9 3.1 copy.335
  33.0 3.2 copy.334
  36.3 9.0 %all-to-all-done.2 = bf16[256,8,256]{2,0,1:T(8,128)(2,1)S(1)} async-done(((bf16[256,8,256]{2,0,1:T(8,128)(2,1)}), bf16[256,8,256]{2,0,1:T(8,128)(2,1)S(1)}, u32[]{:S(2)}, u32[]{:S(2)}) %all-to-all-start.2) | async-done | bytes 1048608 | tf_op jit(solution)/shard_map/all_to_all | solution.py:86
  45.3 4.3 %all-to-all-start.1 = ((bf16[256,8,512]{2,0,1:T(8,128)(2,1)}), bf16[256,8,512]{2,0,1:T(8,128)(2,1)}, u32[]{:S(2)}, u32[]{:S(2)}) async-start(bf16[256,8,512]{2,0,1:T(8,128)(2,1)} %bitcast.303), calls=%async_computation.1 | async-start | bytes 4194304 | tf_op jit(solution)/shard_map/all_to_all | solution.py:84
  61.6 3.3 collective-permute-start.1
  65.0 15.5 %all-to-all-done.1 = bf16[256,8,512]{2,0,1:T(8,128)(2,1)} async-done(((bf16[256,8,512]{2,0,1:T(8,128)(2,1)}), bf16[256,8,512]{2,0,1:T(8,128)(2,1)}, u32[]{:S(2)}, u32[]{:S(2)}) %all-to-all-start.1) | async-done | bytes 2097184 | tf_op jit(solution)/shard_map/all_to_all | solution.py:84
  80.5 4.9 %all-to-all-start.3 = ((bf16[256,8,512]{2,0,1:T(8,128)(2,1)}), bf16[256,8,512]{2,0,1:T(8,128)(2,1)}, u32[]{:S(2)}, u32[]{:S(2)}) async-start(bf16[256,8,512]{2,0,1:T(8,128)(2,1)} %bitcast.302), calls=%async_computation.3 | async-start | bytes 4194304 | tf_op jit(solution)/shard_map/all_to_all | solution.py:87
  87.2 2.7 slice.365
  90.0 3.1 copy.205
  93.0 2.7 slice.373
  95.7 3.1 copy.209
  100.1 2.7 slice.369
  102.8 2.7 slice.377
  110.3 2.7 fusion.152
  117.5 2.9 fusion.153
  127.3 8.2 %fusion.171 = (f32[2,2,512]{2,1,0:T(2,128)S(1)}, f32[2,2,512,1536]{2,3,1,0:T(8,128)}) fusion(pred[512,1536]{0,1:T(8,128)(4,1)} %fusion.41, bf16[3072,2,128]{2,0,1:T(8,128)(2,1)S(1)} %copy-done.10, bf16[512,2,2,128]{3,2,1,0:T(2,128)(2,1)S(1)} %slice.352), kind=kOutput, calls=%fused_computation.192 | convolution fusion | flops 817890816 | bytes 14688256 | tf_op jit(solution)/shard_map/sub | solution.py:34
  135.5 7.7 %fusion.48 = f32[1536,2,128]{2,0,1:T(8,128)} fusion(bf16[512,2,2,128]{3,2,1,0:T(2,128)(2,1)S(1)} %copy-done.25, f32[2,2,512,1536]{2,3,1,0:T(8,128)} %get-tuple-element.157, f32[2,2,512]{2,1,0:T(2,128)S(1)} %get-tuple-element.156), kind=kOutput, calls=%fused_computation.76 | convolution fusion | flops 811597824 | bytes 14688256 | tf_op jit(solution)/shard_map/hgqk,qhgd->khd/dot_general | solution.py:50
  144.6 5.5 %fusion.13 = (f32[2,2,512]{2,1,0:T(2,128)S(1)}, f32[2,1536,512,2]{2,1,3,0:T(8,128)}) fusion(f32[2,2,512,1536]{2,3,1,0:T(8,128)S(1)} %copy-done.5, f32[2,2,512]{2,1,0:T(2,128)S(1)} %get-tuple-element.156, bf16[512,2,2,128]{3,2,1,0:T(2,128)(2,1)S(1)} %copy-done.25, bf16[3072,2,128]{2,0,1:T(8,128)(2,1)S(1)} %copy-done.27), kind=kOutput, calls=%fused_computation.24 | convolution fusion | flops 814741504 | bytes 26492928 | tf_op jit(solution)/shard_map/qhgd,khd->hgqk/dot_general | solution.py:36
  150.1 7.3 %fusion.166 = (f32[2,2,512]{2,1,0:T(2,128)S(1)}, f32[2,2,512,1536]{2,3,1,0:T(8,128)}) fusion(pred[512,1536]{0,1:T(8,128)(4,1)S(1)} %copy-done.21, bf16[3072,2,128]{2,0,1:T(8,128)(2,1)S(1)} %copy-done.10, bf16[512,2,2,128]{3,2,1,0:T(2,128)(2,1)S(1)} %slice.360), kind=kOutput, calls=%fused_computation.191 | convolution fusion | flops 817890816 | bytes 14688256 | tf_op jit(solution)/shard_map/sub | solution.py:34
  159.3 11.5 %fusion.10 = (f32[2,2,512]{2,1,0:T(2,128)S(1)}, f32[2,1536,512,2]{2,1,3,0:T(8,128)}) fusion(f32[2,2,512,1536]{2,3,1,0:T(8,128)} %get-tuple-element.153, f32[2,2,512]{2,1,0:T(2,128)S(1)} %get-tuple-element.152, bf16[512,2,2,128]{3,2,1,0:T(2,128)(2,1)} %slice.363, bf16[3072,2,128]{2,0,1:T(8,128)(2,1)} %copy-done.26), kind=kOutput, calls=%fused_computation.18 | convolution fusion | flops 814741504 | bytes 26492928 | tf_op jit(solution)/shard_map/qhgd,khd->hgqk/dot_general | solution.py:36
  173.0 10.6 %fusion.161 = (f32[2,2,512]{2,1,0:T(2,128)S(1)}, f32[2,2,512,1536]{2,3,1,0:T(8,128)}) fusion(pred[512,1536]{0,1:T(8,128)(4,1)} %fusion.45, bf16[1536,2,128,1]{0,2,3,1:T(8,128)(2,1)} %copy.205, bf16[512,2,2,128]{3,2,1,0:T(2,128)(2,1)} %slice.367), kind=kOutput, calls=%fused_computation.190 | convolution fusion | flops 817890816 | bytes 14688256 | tf_op jit(solution)/shard_map/sub | solution.py:34
  183.5 12.0 %fusion.7 = (f32[2,2,512]{2,1,0:T(2,128)S(1)}, f32[2,1536,512,2]{2,1,3,0:T(8,128)}) fusion(f32[2,2,512,1536]{2,3,1,0:T(8,128)} %get-tuple-element.149, f32[2,2,512]{2,1,0:T(2,128)S(1)} %get-tuple-element.148, bf16[512,2,2,128]{3,2,1,0:T(2,128)(2,1)} %slice.371, bf16[1536,2,128,1]{2,1,0,3:T(2,128)(2,1)} %bitcast.321), kind=kOutput, calls=%fused_computation.12 | convolution fusion | flops 814741504 | bytes 26492928 | tf_op jit(solution)/shard_map/qhgd,khd->hgqk/dot_general | solution.py:36
  195.5 2.4 fusion.66
  197.9 10.6 %fusion.156 = (f32[2,2,512]{2,1,0:T(2,128)S(1)}, f32[2,2,512,1536]{2,3,1,0:T(8,128)}) fusion(pred[512,1536]{0,1:T(8,128)(4,1)} %fusion.47, bf16[1536,2,128,1]{0,2,3,1:T(8,128)(2,1)} %copy.209, bf16[512,2,2,128]{3,2,1,0:T(2,128)(2,1)} %slice.375), kind=kOutput, calls=%fused_computation.189 | convolution fusion | flops 817890816 | bytes 14688256 | tf_op jit(solution)/shard_map/sub | solution.py:34
  208.5 11.5 %fusion.4 = (f32[2,2,512]{2,1,0:T(2,128)S(1)}, f32[2,1536,512,2]{2,1,3,0:T(8,128)}) fusion(f32[2,2,512,1536]{2,3,1,0:T(8,128)} %get-tuple-element.145, f32[2,2,512]{2,1,0:T(2,128)S(1)} %get-tuple-element.144, bf16[512,2,2,128]{3,2,1,0:T(2,128)(2,1)} %slice.379, bf16[1536,2,128,1]{2,1,0,3:T(2,128)(2,1)} %bitcast.320), kind=kOutput, calls=%fused_computation.6 | convolution fusion | flops 814741504 | bytes 26492928 | tf_op jit(solution)/shard_map/qhgd,khd->hgqk/dot_general | solution.py:36
  220.0 6.6 %fusion.72 = f32[1536,2,128]{2,0,1:T(8,128)S(1)} fusion(f32[3072,2,128]{2,0,1:T(8,128)S(1)} %fusion.66, bf16[512,2,2,128]{3,2,1,0:T(2,128)(2,1)S(1)} %copy-done.22, f32[2,2,512,1536]{2,3,1,0:T(8,128)} %get-tuple-element.145, f32[2,2,512]{2,1,0:T(2,128)S(1)} %get-tuple-element.144), kind=kOutput, calls=%fused_computation.84 | convolution fusion | flops 811991040 | bytes 16261120 | tf_op jit(solution)/shard_map/hgqk,qhgd->khd/dot_general | solution.py:50
  228.2 7.1 %fusion.15 = bf16[2,2,512,1536]{2,3,1,0:T(8,128)(2,1)S(1)} fusion(f32[2,1536,512,2]{2,1,3,0:T(8,128)} %get-tuple-element.159, f32[2,2,512]{2,1,0:T(2,128)S(1)} %get-tuple-element.158, f32[2,2,512,1536]{2,3,1,0:T(8,128)S(1)} %bitcast.301, f32[2,2,512]{2,1,0:T(2,128)S(1)} %get-tuple-element.156), kind=kLoop, calls=%fused_computation.26 | loop fusion | flops 12582912 | bytes 31473664 | tf_op jit(solution)/shard_map/convert_element_type | solution.py:40
  238.0 9.6 %fusion.9 = bf16[2,2,512,1536]{2,3,1,0:T(8,128)(2,1)S(1)} fusion(f32[2,1536,512,2]{2,1,3,0:T(8,128)} %get-tuple-element.151, f32[2,2,512]{2,1,0:T(2,128)S(1)} %get-tuple-element.150, f32[2,2,512,1536]{2,3,1,0:T(8,128)} %get-tuple-element.149, f32[2,2,512]{2,1,0:T(2,128)S(1)} %get-tuple-element.148), kind=kLoop, calls=%fused_computation.14 | loop fusion | flops 12582912 | bytes 31473664 | tf_op jit(solution)/shard_map/convert_element_type | solution.py:40
  247.6 11.9 %fusion.6 = bf16[2,2,512,1536]{2,3,1,0:T(8,128)(2,1)S(1)} fusion(f32[2,1536,512,2]{2,1,3,0:T(8,128)} %get-tuple-element.147, f32[2,2,512]{2,1,0:T(2,128)S(1)} %get-tuple-element.146, f32[2,2,512,1536]{2,3,1,0:T(8,128)} %get-tuple-element.145, f32[2,2,512]{2,1,0:T(2,128)S(1)} %get-tuple-element.144), kind=kLoop, calls=%fused_computation.8 | loop fusion | flops 12582912 | bytes 31473664 | tf_op jit(solution)/shard_map/convert_element_type | solution.py:40
  259.6 11.9 %fusion.12 = bf16[2,2,512,1536]{2,3,1,0:T(8,128)(2,1)S(1)} fusion(f32[2,1536,512,2]{2,1,3,0:T(8,128)} %get-tuple-element.155, f32[2,2,512]{2,1,0:T(2,128)S(1)} %get-tuple-element.154, f32[2,2,512,1536]{2,3,1,0:T(8,128)} %get-tuple-element.153, f32[2,2,512]{2,1,0:T(2,128)S(1)} %get-tuple-element.152), kind=kLoop, calls=%fused_computation.20 | loop fusion | flops 12582912 | bytes 31473664 | tf_op jit(solution)/shard_map/convert_element_type | solution.py:40
  286.3 7.3 %all-to-all-start.6 = ((bf16[8,256,256]{1,2,0:T(8,128)(2,1)}), bf16[8,256,256]{1,2,0:T(8,128)(2,1)S(1)}, u32[]{:S(2)}, u32[]{:S(2)}) async-start(bf16[8,256,256]{1,2,0:T(8,128)(2,1)} %copy.190), calls=%async_computation.6 | async-start | bytes 2097152 | tf_op jit(solution)/shard_map/all_to_all | solution.py:119
  293.7 5.0 %fusion.98 = bf16[2,2,512,128]{2,3,1,0:T(8,128)(2,1)} fusion(bf16[1536,2,128,1]{0,2,3,1:T(8,128)(2,1)} %copy.205, bf16[2,2,512,1536]{2,3,1,0:T(8,128)(2,1)} %copy-done.2), kind=kOutput, calls=%fused_computation.115 | convolution fusion | flops 805830656 | bytes 7602176 | tf_op jit(solution)/shard_map/hgqk,khd->qhgd/dot_general | solution.py:43
  298.6 2.8 slice.412
  308.3 2.9 all-to-all-done.6
  311.2 4.4 %all-to-all-start.5 = ((bf16[8,256,256]{1,2,0:T(8,128)(2,1)}), bf16[8,256,256]{1,2,0:T(8,128)(2,1)}, u32[]{:S(2)}, u32[]{:S(2)}) async-start(bf16[8,256,256]{1,2,0:T(8,128)(2,1)} %copy.184), calls=%async_computation.5 | async-start | bytes 2097152 | tf_op jit(solution)/shard_map/all_to_all | solution.py:118
  315.6 4.2 %fusion.99 = bf16[2,2,512,128]{2,3,1,0:T(8,128)(2,1)S(1)} fusion(bf16[1536,2,128,1]{0,2,3,1:T(8,128)(2,1)} %copy.209, bf16[2,2,512,1536]{2,3,1,0:T(8,128)(2,1)} %copy-done.1), kind=kOutput, calls=%fused_computation.116 | convolution fusion | flops 805830656 | bytes 7602176 | tf_op jit(solution)/shard_map/hgqk,khd->qhgd/dot_general | solution.py:43
  321.6 2.5 copy.177
  324.1 10.0 %all-to-all-done.5 = bf16[8,256,256]{1,2,0:T(8,128)(2,1)} async-done(((bf16[8,256,256]{1,2,0:T(8,128)(2,1)}), bf16[8,256,256]{1,2,0:T(8,128)(2,1)}, u32[]{:S(2)}, u32[]{:S(2)}) %all-to-all-start.5) | async-done | bytes 1048608 | tf_op jit(solution)/shard_map/all_to_all | solution.py:118
  334.2 4.4 %all-to-all-start.4 = ((bf16[8,256,512]{2,1,0:T(8,128)(2,1)}), bf16[8,256,512]{2,1,0:T(8,128)(2,1)S(1)}, u32[]{:S(2)}, u32[]{:S(2)}) async-start(bf16[8,256,512]{2,1,0:T(8,128)(2,1)} %bitcast.36), calls=%async_computation.4 | async-start | bytes 4194304 | tf_op jit(solution)/shard_map/all_to_all | solution.py:117
  340.0 2.3 copy.192
  342.2 27.8 %all-to-all-done.4 = bf16[8,256,512]{2,1,0:T(8,128)(2,1)S(1)} async-done(((bf16[8,256,512]{2,1,0:T(8,128)(2,1)}), bf16[8,256,512]{2,1,0:T(8,128)(2,1)S(1)}, u32[]{:S(2)}, u32[]{:S(2)}) %all-to-all-start.4) | async-done | bytes 2097184 | tf_op jit(solution)/shard_map/all_to_all | solution.py:117
  370.0 2.4 copy.178
  372.4 4.1 %copy.191 = bf16[256,4096]{1,0:T(8,128)(2,1)} copy(bf16[256,4096]{0,1:T(8,128)(2,1)} %bitcast.304) | data formatting | bytes 4194304
  (150 shorter events, 65.6 us)
Async XLA Ops:
  2.9 23.0 %all-to-all-start = ((bf16[256,8,256]{2,0,1:T(8,128)(2,1)}), bf16[256,8,256]{2,0,1:T(8,128)(2,1)S(1)}, u32[]{:S(2)}, u32[]{:S(2)}) async-start(bf16[256,8,256]{2,0,1:T(8,128)(2,1)} %bitcast.287), calls=%async_computation | async-start | bytes 2097152 | tf_op jit(solution)/shard_map/all_to_all | solution.py:85
  25.8 19.4 %all-to-all-start.2 = ((bf16[256,8,256]{2,0,1:T(8,128)(2,1)}), bf16[256,8,256]{2,0,1:T(8,128)(2,1)S(1)}, u32[]{:S(2)}, u32[]{:S(2)}) async-start(bf16[256,8,256]{2,0,1:T(8,128)(2,1)} %bitcast.286), calls=%async_computation.2 | async-start | bytes 2097152 | tf_op jit(solution)/shard_map/all_to_all | solution.py:86
  45.3 35.2 %all-to-all-start.1 = ((bf16[256,8,512]{2,0,1:T(8,128)(2,1)}), bf16[256,8,512]{2,0,1:T(8,128)(2,1)}, u32[]{:S(2)}, u32[]{:S(2)}) async-start(bf16[256,8,512]{2,0,1:T(8,128)(2,1)} %bitcast.303), calls=%async_computation.1 | async-start | bytes 4194304 | tf_op jit(solution)/shard_map/all_to_all | solution.py:84
  58.5 47.0 %collective-permute-start = (bf16[1024,2,128]{2,0,1:T(8,128)(2,1)}, bf16[1024,2,128]{2,0,1:T(8,128)(2,1)}, u32[]{:S(2)}, u32[]{:S(2)}) collective-permute-start(bf16[1024,2,128]{2,0,1:T(8,128)(2,1)} %copy.148), channel_id=1, source_target_pairs={{0,8},{8,16},{16,24},{24,32},{32,40},{40,48},{48,56},{56,64},{64,7... | collective-permute-start | bytes 1572872 | tf_op jit(solution)/shard_map/ppermute | solution.py:19
  61.6 44.9 %collective-permute-start.1 = (bf16[1024,2,128]{2,0,1:T(8,128)(2,1)}, bf16[1024,2,128]{2,0,1:T(8,128)(2,1)}, u32[]{:S(2)}, u32[]{:S(2)}) collective-permute-start(bf16[1024,2,128]{2,0,1:T(8,128)(2,1)} %copy.154), channel_id=1, source_target_pairs={{0,8},{8,16},{16,24},{24,32},{32,40},{40,48},{48,56},{56,64},{64,7... | collective-permute-start | bytes 1572872 | tf_op jit(solution)/shard_map/ppermute | solution.py:19
  80.5 37.0 %all-to-all-start.3 = ((bf16[256,8,512]{2,0,1:T(8,128)(2,1)}), bf16[256,8,512]{2,0,1:T(8,128)(2,1)}, u32[]{:S(2)}, u32[]{:S(2)}) async-start(bf16[256,8,512]{2,0,1:T(8,128)(2,1)} %bitcast.302), calls=%async_computation.3 | async-start | bytes 4194304 | tf_op jit(solution)/shard_map/all_to_all | solution.py:87
  109.1 1.2 copy-start.26
  113.0 14.3 %copy-start.10 = (bf16[3072,2,128]{2,0,1:T(8,128)(2,1)S(1)}, bf16[3072,2,128]{2,0,1:T(8,128)(2,1)}, u32[]{:S(2)}) copy-start(bf16[3072,2,128]{2,0,1:T(8,128)(2,1)} %copy-done.9) | copy-start | bytes 4718596
  114.3 21.2 %copy-start.17 = (bf16[512,2,2,128]{3,2,1,0:T(2,128)(2,1)}, bf16[512,2,2,128]{3,2,1,0:T(2,128)(2,1)S(1)}, u32[]{:S(2)}) copy-start(bf16[512,2,2,128]{3,2,1,0:T(2,128)(2,1)S(1)} %slice.352) | copy-start | bytes 1572868
  117.5 32.6 %copy-start.15 = (bf16[512,2,2,128]{3,2,1,0:T(2,128)(2,1)}, bf16[512,2,2,128]{3,2,1,0:T(2,128)(2,1)S(1)}, u32[]{:S(2)}) copy-start(bf16[512,2,2,128]{3,2,1,0:T(2,128)(2,1)S(1)} %slice.360) | copy-start | bytes 1572868
  127.3 8.2 %copy-start.25 = (bf16[512,2,2,128]{3,2,1,0:T(2,128)(2,1)S(1)}, bf16[512,2,2,128]{3,2,1,0:T(2,128)(2,1)}, u32[]{:S(2)}) copy-start(bf16[512,2,2,128]{3,2,1,0:T(2,128)(2,1)} %slice.357) | copy-start | bytes 1572868
  135.5 8.7 %copy-start.5 = (f32[2,2,512,1536]{2,3,1,0:T(8,128)S(1)}, f32[2,2,512,1536]{2,3,1,0:T(8,128)}, u32[]{:S(2)}) copy-start(f32[2,2,512,1536]{2,3,1,0:T(8,128)} %get-tuple-element.157) | copy-start | bytes 37748740
  135.5 9.1 %copy-start.27 = (bf16[3072,2,128]{2,0,1:T(8,128)(2,1)S(1)}, bf16[3072,2,128]{2,0,1:T(8,128)(2,1)}, u32[]{:S(2)}) copy-start(bf16[3072,2,128]{2,0,1:T(8,128)(2,1)} %copy-done.26) | copy-start | bytes 4718596
  144.6 5.5 %copy-start.21 = (pred[512,1536]{0,1:T(8,128)(4,1)S(1)}, pred[512,1536]{0,1:T(8,128)(4,1)}, u32[]{:S(2)}) copy-start(pred[512,1536]{0,1:T(8,128)(4,1)} %fusion.43) | copy-start | bytes 2359300
  157.5 13.3 %slice-start.4 = ((s8[12582912]{0:T(1024)(128)(4,1)}), s8[4194304]{0:T(1024)(128)(4,1)S(1)}, s32[]{:S(2)}) async-start(s8[12582912]{0:T(1024)(128)(4,1)} %bitcast.298), calls=%async_computation.11 | async-start | bytes 8388608
  159.2 11.5 %slice-start.5 = ((s8[12582912]{0:T(1024)(128)(4,1)}), s8[4194304]{0:T(1024)(128)(4,1)S(1)}, s32[]{:S(2)}) async-start(s8[12582912]{0:T(1024)(128)(4,1)} %bitcast.298), calls=%async_computation.12 | async-start | bytes 8388608
  159.2 11.5 %slice-start.6 = ((s8[12582912]{0:T(1024)(128)(4,1)}), s8[4194304]{0:T(1024)(128)(4,1)S(1)}, s32[]{:S(2)}) async-start(s8[12582912]{0:T(1024)(128)(4,1)} %bitcast.298), calls=%async_computation.13 | async-start | bytes 8388608
  159.3 11.5 %copy-start.24 = (bf16[512,2,2,128]{3,2,1,0:T(2,128)(2,1)S(1)}, bf16[512,2,2,128]{3,2,1,0:T(2,128)(2,1)}, u32[]{:S(2)}) copy-start(bf16[512,2,2,128]{3,2,1,0:T(2,128)(2,1)} %slice.363) | copy-start | bytes 1572868
  183.5 12.0 %copy-start.6 = (f32[2,2,512,1536]{2,3,1,0:T(8,128)S(1)}, f32[2,2,512,1536]{2,3,1,0:T(8,128)}, u32[]{:S(2)}) copy-start(f32[2,2,512,1536]{2,3,1,0:T(8,128)} %get-tuple-element.149) | copy-start | bytes 37748740
  183.5 12.0 %copy-start.23 = (bf16[512,2,2,128]{3,2,1,0:T(2,128)(2,1)S(1)}, bf16[512,2,2,128]{3,2,1,0:T(2,128)(2,1)}, u32[]{:S(2)}) copy-start(bf16[512,2,2,128]{3,2,1,0:T(2,128)(2,1)} %slice.371) | copy-start | bytes 1572868
  208.5 11.5 %copy-start.22 = (bf16[512,2,2,128]{3,2,1,0:T(2,128)(2,1)S(1)}, bf16[512,2,2,128]{3,2,1,0:T(2,128)(2,1)}, u32[]{:S(2)}) copy-start(bf16[512,2,2,128]{3,2,1,0:T(2,128)(2,1)} %slice.379) | copy-start | bytes 1572868
  208.5 19.6 %slice-start.7 = ((s8[12582912]{0:T(1024)(128)(4,1)}), s8[4194304]{0:T(1024)(128)(4,1)S(1)}, s32[]{:S(2)}) async-start(s8[12582912]{0:T(1024)(128)(4,1)} %bitcast.300), calls=%async_computation.14 | async-start | bytes 8388608
  208.5 19.6 %slice-start.8 = ((s8[12582912]{0:T(1024)(128)(4,1)}), s8[4194304]{0:T(1024)(128)(4,1)S(1)}, s32[]{:S(2)}) async-start(s8[12582912]{0:T(1024)(128)(4,1)} %bitcast.300), calls=%async_computation.15 | async-start | bytes 8388608
  220.0 8.1 %slice-start.9 = ((s8[12582912]{0:T(1024)(128)(4,1)}), s8[4194304]{0:T(1024)(128)(4,1)S(1)}, s32[]{:S(2)}) async-start(s8[12582912]{0:T(1024)(128)(4,1)} %bitcast.300), calls=%async_computation.16 | async-start | bytes 8388608
  226.8 55.5 %collective-permute-start.3 = (bf16[1024,2,128]{2,0,1:T(8,128)(2,1)S(1)}, bf16[1024,2,128]{2,0,1:T(8,128)(2,1)S(1)}, u32[]{:S(2)}, u32[]{:S(2)}) collective-permute-start(bf16[1024,2,128]{2,0,1:T(8,128)(2,1)S(1)} %slice.454), channel_id=1, source_target_pairs={{8,0},{16,8},{24,16},{32,24},{40,32},{48,40},{56,48},{64,56},{72,6... | collective-permute-start | bytes 1572872 | tf_op jit(solution)/shard_map/ppermute | solution.py:19
  228.1 7.2 %copy-start.18 = (bf16[512,2,2,128]{3,2,1,0:T(2,128)(2,1)S(1)}, bf16[512,2,2,128]{3,2,1,0:T(2,128)(2,1)}, u32[]{:S(2)}) copy-start(bf16[512,2,2,128]{3,2,1,0:T(2,128)(2,1)} %copy-done.17) | copy-start | bytes 1572868
  235.3 2.7 copy-start
  247.6 25.7 %copy-start.2 = (bf16[2,2,512,1536]{2,3,1,0:T(8,128)(2,1)}, bf16[2,2,512,1536]{2,3,1,0:T(8,128)(2,1)S(1)}, u32[]{:S(2)}) copy-start(bf16[2,2,512,1536]{2,3,1,0:T(8,128)(2,1)S(1)} %fusion.9) | copy-start | bytes 18874372
  259.5 15.7 %copy-start.1 = (bf16[2,2,512,1536]{2,3,1,0:T(8,128)(2,1)}, bf16[2,2,512,1536]{2,3,1,0:T(8,128)(2,1)S(1)}, u32[]{:S(2)}) copy-start(bf16[2,2,512,1536]{2,3,1,0:T(8,128)(2,1)S(1)} %fusion.6) | copy-start | bytes 18874372
  259.6 11.9 %copy-start.16 = (bf16[512,2,2,128]{3,2,1,0:T(2,128)(2,1)S(1)}, bf16[512,2,2,128]{3,2,1,0:T(2,128)(2,1)}, u32[]{:S(2)}) copy-start(bf16[512,2,2,128]{3,2,1,0:T(2,128)(2,1)} %copy-done.15) | copy-start | bytes 1572868
  271.5 3.7 copy-start.3
  271.5 1.9 copy-start.14
  273.4 1.9 copy-start.13
  277.1 3.9 %copy-start.7 = (f32[1536,2,128]{2,0,1:T(8,128)}, f32[1536,2,128]{2,0,1:T(8,128)S(1)}, u32[]{:S(2)}) copy-start(f32[1536,2,128]{2,0,1:T(8,128)S(1)} %fusion.77) | copy-start | bytes 4718596
  278.4 1.7 copy-start.4
  281.0 22.3 %collective-permute-start.2 = (bf16[1024,2,128]{2,0,1:T(8,128)(2,1)}, bf16[1024,2,128]{2,0,1:T(8,128)(2,1)}, u32[]{:S(2)}, u32[]{:S(2)}) collective-permute-start(bf16[1024,2,128]{2,0,1:T(8,128)(2,1)} %slice.455), channel_id=1, source_target_pairs={{8,0},{16,8},{24,16},{32,24},{40,32},{48,40},{56,48},{64,56},{72,6... | collective-permute-start | bytes 1572872 | tf_op jit(solution)/shard_map/ppermute | solution.py:19
  286.3 15.1 %slice-start.2 = ((s8[6291456]{0:T(1024)(128)(4,1)}), s8[2097152]{0:T(1024)(128)(4,1)S(1)}, s32[]{:S(2)}) async-start(s8[6291456]{0:T(1024)(128)(4,1)} %bitcast.290), calls=%async_computation.9 | async-start | bytes 4194304
  286.3 24.8 %all-to-all-start.6 = ((bf16[8,256,256]{1,2,0:T(8,128)(2,1)}), bf16[8,256,256]{1,2,0:T(8,128)(2,1)S(1)}, u32[]{:S(2)}, u32[]{:S(2)}) async-start(bf16[8,256,256]{1,2,0:T(8,128)(2,1)} %copy.190), calls=%async_computation.6 | async-start | bytes 2097152 | tf_op jit(solution)/shard_map/all_to_all | solution.py:119
  293.6 7.8 %slice-start.3 = ((s8[6291456]{0:T(1024)(128)(4,1)}), s8[4194304]{0:T(1024)(128)(4,1)S(1)}, s32[]{:S(2)}) async-start(s8[6291456]{0:T(1024)(128)(4,1)} %bitcast.290), calls=%async_computation.10 | async-start | bytes 8388608
  293.6 7.8 %copy-start.11 = (bf16[3072,2,128]{2,0,1:T(8,128)(2,1)S(1)}, bf16[3072,2,128]{2,0,1:T(8,128)(2,1)}, u32[]{:S(2)}) copy-start(bf16[3072,2,128]{2,0,1:T(8,128)(2,1)} %copy-done.9) | copy-start | bytes 4718596
  298.6 4.7 %copy-start.8 = (f32[1536,2,128]{2,0,1:T(8,128)S(1)}, f32[1536,2,128]{2,0,1:T(8,128)}, u32[]{:S(2)}) copy-start(f32[1536,2,128]{2,0,1:T(8,128)} %copy-done.7) | copy-start | bytes 4718596
  307.1 12.7 %slice-start = ((s8[6291456]{0:T(1024)(128)(4,1)}), s8[2097152]{0:T(1024)(128)(4,1)S(1)}, s32[]{:S(2)}) async-start(s8[6291456]{0:T(1024)(128)(4,1)} %bitcast.288), calls=%async_computation.7 | async-start | bytes 4194304
  311.2 23.0 %all-to-all-start.5 = ((bf16[8,256,256]{1,2,0:T(8,128)(2,1)}), bf16[8,256,256]{1,2,0:T(8,128)(2,1)}, u32[]{:S(2)}, u32[]{:S(2)}) async-start(bf16[8,256,256]{1,2,0:T(8,128)(2,1)} %copy.184), calls=%async_computation.5 | async-start | bytes 2097152 | tf_op jit(solution)/shard_map/all_to_all | solution.py:118
  315.5 4.2 %slice-start.1 = ((s8[6291456]{0:T(1024)(128)(4,1)}), s8[4194304]{0:T(1024)(128)(4,1)S(1)}, s32[]{:S(2)}) async-start(s8[6291456]{0:T(1024)(128)(4,1)} %bitcast.288), calls=%async_computation.8 | async-start | bytes 8388608
  315.5 4.7 %copy-start.12 = (bf16[3072,2,128]{2,0,1:T(8,128)(2,1)S(1)}, bf16[3072,2,128]{2,0,1:T(8,128)(2,1)}, u32[]{:S(2)}) copy-start(bf16[3072,2,128]{2,0,1:T(8,128)(2,1)} %copy-done.9) | copy-start | bytes 4718596
  315.6 5.8 %copy-start.19 = (bf16[2,2,512,128]{2,3,1,0:T(8,128)(2,1)S(1)}, bf16[2,2,512,128]{2,3,1,0:T(8,128)(2,1)}, u32[]{:S(2)}) copy-start(bf16[2,2,512,128]{2,3,1,0:T(8,128)(2,1)} %fusion.98) | copy-start | bytes 1572868
  315.6 5.8 %copy-start.20 = (bf16[2,128,2,512]{3,1,2,0:T(8,128)(2,1)S(1)}, bf16[2,128,2,512]{3,1,2,0:T(8,128)(2,1)}, u32[]{:S(2)}) copy-start(bf16[2,128,2,512]{3,1,2,0:T(8,128)(2,1)} %fusion.97) | copy-start | bytes 1572868
  334.2 35.9 %all-to-all-start.4 = ((bf16[8,256,512]{2,1,0:T(8,128)(2,1)}), bf16[8,256,512]{2,1,0:T(8,128)(2,1)S(1)}, u32[]{:S(2)}, u32[]{:S(2)}) async-start(bf16[8,256,512]{2,1,0:T(8,128)(2,1)} %bitcast.36), calls=%async_computation.4 | async-start | bytes 4194304 | tf_op jit(solution)/shard_map/all_to_all | solution.py:117
  (1 other events, 1.1 us)
where the time goes:
time: 382 us; the launch traced here: 377 us
  matrix products  115 us (30%)
  local copies, waits for them, and re-layouts  85 us (22%)
  waiting for transfers between devices  78.8 us (21%)
  other arithmetic  51.6 us (14%)
  starting transfers between devices  44.4 us (12%)
    convert_element_type x4, other arithmetic, block_grads(): score_grad = (probability * (prob_grad - row_centre)).astype(jnp.bfloat16)  40.6 us
    dot_general x4, matrix products, block_grads(): jnp.einsum('qhgd,khd->hgqk', grad_block, value_block, preferred_element_t...  40.5 us
    sub x4, matrix products, block_grads(): raised = jnp.exp(scores - row_peak)  36.6 us
    all_to_all x1, waiting for transfers between devices, local(): lax.all_to_all(outgoing[0], 'head', split_axis=0, concat_axis=1, tiled=True)  27.8 us
    dot_general x4, matrix products, block_grads(): jnp.einsum('hgqk,qhgd->khd', prob_low, grad_block, preferred_element_type...  18.8 us
    unnamed x83, local copies, waits for them, and re-layouts  17 us
    all_to_all x1, waiting for transfers between devices, local(): lax.all_to_all(queries, 'head', split_axis=1, concat_axis=0, tiled=True)  15.5 us
    all_to_all x1, waiting for transfers between devices, local(): lax.all_to_all(key_rows, 'head', split_axis=1, concat_axis=0, tiled=True)  13.6 us
  transfers between devices with their start and end apart: 11, of which 6 were waited for; matrix products, arithmetic and copies ran while one was open for 34% of the time, Pallas kernels for 0%

commit v1 on v0

v1 whole, which is shorter than its diff:
```python
import functools
import math

import jax
import jax.numpy as jnp
from jax import lax
from jax.experimental import pallas as pl
from jax.experimental.pallas import tpu as pltpu
from jax.sharding import PartitionSpec as P

HEAD_DIM = 128
WINDOW = 1024
GROUP = 2
SCALE = 168.0 ** (-0.5)
LOG2E = math.log2(math.e)
NEG = -1e30

ROWS = 256
HALO = WINDOW // ROWS
SPAN = HALO + 1
HEADS_KV = 2
PAIR = GROUP * HEAD_DIM
MESH = pl.DeviceIdType.MESH
PEERS = ((2, 1), (1, 1), (3, 1), (2, 0), (0, 1), (1, 0), (3, 0))


def rows_of(index, count):
    return pl.ds(pl.multiple_of(index * count, count), count)


def fold(op, value):
    out = value[0:8]
    for begin in range(8, value.shape[0], 8):
        out = op(out, value[begin : begin + 8])
    return out


def kernel(
    seq_count,
    q_hbm,
    k_hbm,
    v_hbm,
    g_hbm,
    dq_hbm,
    dk_hbm,
    dv_hbm,
    qg,
    kv,
    dkv,
    dkv_low,
    halo_in,
    dq_low,
    s_buf,
    g_buf,
    p_low,
    s_low,
    qg_sem,
    kv_sem,
    in_send,
    halo_send,
    halo_recv,
    back_send,
    back_recv,
    out_send,
    out_recv,
    own_sem,
):
    s, h = lax.axis_index("seq"), lax.axis_index("head")
    x, y = h // 2, lax.rem(h, 2)
    after = (lax.rem(s + 1, seq_count), h)
    before = (lax.rem(s + seq_count - 1, seq_count), h)
    peers = []
    for dx, dy in PEERS:
        across = lax.rem(y + dy, 2)
        peers.append(lax.rem(x + dx, 4) * 2 + across)

    barrier = pltpu.get_barrier_semaphore()
    for peer in peers:
        pl.semaphore_signal(barrier, inc=1, device_id=(s, peer), device_id_type=MESH)
    for device in (after, before):
        pl.semaphore_signal(barrier, inc=1, device_id=device, device_id_type=MESH)
    pl.semaphore_wait(barrier, len(PEERS) + 2)

    def kv_parts(j, owner):
        col = pl.multiple_of((owner * HEADS_KV + j) * HEAD_DIM, HEAD_DIM)
        for part, ref in enumerate((k_hbm, v_hbm)):
            yield (
                ref.at[:, pl.ds(col, HEAD_DIM)],
                kv.at[j, HALO + h, :, part * HEAD_DIM : (part + 1) * HEAD_DIM],
            )

    def qg_parts(j, owner, piece):
        col = pl.multiple_of((owner * HEADS_KV + j) * PAIR, PAIR)
        half = slice(piece * (ROWS // 2), (piece + 1) * (ROWS // 2))
        for part, ref in enumerate((q_hbm, g_hbm)):
            yield (
                ref.at[half, pl.ds(col, PAIR)],
                qg.at[j, h, half, part * PAIR : (part + 1) * PAIR],
            )

    def push(src, dst, send, recv, device):
        pltpu.make_async_remote_copy(
            src_ref=src, dst_ref=dst, send_sem=send, recv_sem=recv, device_id=device, device_id_type=MESH
        ).start()

    def push_kv(j):
        for part in range(2):
            for n, peer in enumerate(peers):
                src, dst = list(kv_parts(j, peer))[part]
                push(src, dst, in_send.at[n], kv_sem.at[j, h], (s, peer))

    def push_qg(j):
        for piece in range(2):
            for part in range(2):
                for n, peer in enumerate(peers):
                    src, dst = list(qg_parts(j, peer, piece))[part]
                    push(src, dst, in_send.at[n], qg_sem.at[j, h], (s, peer))

    def got(ref, sem):
        pltpu.make_async_copy(ref, ref, sem).wait()

    push_kv(0)
    push_kv(1)
    push_qg(0)
    for j in range(HEADS_KV):
        for src, dst in kv_parts(j, h):
            pltpu.make_async_copy(src, dst, kv_sem.at[j, h]).start()
        for piece in range(2):
            for src, dst in qg_parts(j, h, piece):
                pltpu.make_async_copy(src, dst, qg_sem.at[j, h]).start()

    def clear(b, carry):
        for j in range(HEADS_KV):
            dkv[j, b] = jnp.zeros((ROWS, 2 * HEAD_DIM), jnp.float32)
        return carry

    lax.fori_loop(0, 3 * HALO, clear, 0)

    for j in range(HEADS_KV):
        for r in range(8):
            got(kv.at[j, HALO + r], kv_sem.at[j, r])
        for b in range(HALO):
            push(kv.at[j, 8 + b], kv.at[j, b], halo_send.at[j], halo_recv.at[j], after)
    push_qg(1)

    key_row = lax.broadcasted_iota(jnp.int32, (ROWS, ROWS), 0)
    query_col = lax.broadcasted_iota(jnp.int32, (ROWS, ROWS), 1)

    def unit(j, r):
        keys = kv[j, pl.ds(r, SPAN), :, 0:HEAD_DIM].reshape(SPAN * ROWS, HEAD_DIM)
        values = kv[j, pl.ds(r, SPAN), :, HEAD_DIM:].reshape(SPAN * ROWS, HEAD_DIM)
        for hh in range(GROUP):
            query = qg[j, r, :, hh * HEAD_DIM : (hh + 1) * HEAD_DIM]
            grad = qg[j, r, :, PAIR + hh * HEAD_DIM : PAIR + (hh + 1) * HEAD_DIM]
            nt = (((1,), (1,)), ((), ()))
            s_buf[...] = lax.dot_general(keys, query, nt, preferred_element_type=jnp.float32)
            g_buf[...] = lax.dot_general(values, grad, nt, preferred_element_type=jnp.float32)
            peak = jnp.full((8, ROWS), NEG, jnp.float32)
            for c in range(SPAN):
                part = s_buf[c * ROWS : (c + 1) * ROWS]
                if c < HALO:
                    inside = (s > 0) | (r + c >= HALO)
                    if c == 0:
                        part = jnp.where((key_row > query_col) & inside, part, NEG)
                    else:
                        part = jnp.where(inside, part, NEG)
                else:
                    part = jnp.where(key_row <= query_col, part, NEG)
                s_buf[c * ROWS : (c + 1) * ROWS] = part
                peak = jnp.maximum(peak, fold(jnp.maximum, part))
            peak = jnp.max(peak, axis=0, keepdims=True)
            total = jnp.zeros((8, ROWS), jnp.float32)
            centre = jnp.zeros((8, ROWS), jnp.float32)
            step = 64
            for begin in range(0, SPAN * ROWS, step):
                at = slice(begin, begin + step)
                raised = jnp.exp2((s_buf[at] - peak) * (SCALE * LOG2E))
                s_buf[at] = raised
                total = total + fold(jnp.add, raised)
                centre = centre + fold(jnp.add, raised * g_buf[at])
            scale = 1.0 / jnp.sum(total, axis=0, keepdims=True)
            centre = jnp.sum(centre, axis=0, keepdims=True) * scale
            for begin in range(0, SPAN * ROWS, step):
                at = slice(begin, begin + step)
                prob = s_buf[at] * scale
                p_low[at] = prob.astype(jnp.bfloat16)
                s_low[at] = (prob * (g_buf[at] - centre)).astype(jnp.bfloat16)
            nn = (((1,), (0,)), ((), ()))
            key_part = lax.dot_general(s_low[...], query, nn, preferred_element_type=jnp.float32)
            value_part = lax.dot_general(p_low[...], grad, nn, preferred_element_type=jnp.float32)
            for c in range(SPAN):
                at = slice(c * ROWS, (c + 1) * ROWS)
                dkv[j, r + c, :, 0:HEAD_DIM] += key_part[at]
                dkv[j, r + c, :, HEAD_DIM:] += value_part[at]
            query_part = lax.dot_general(
                s_low[...], keys, (((0,), (0,)), ((), ())), preferred_element_type=jnp.float32
            )
            dq_low[j, r, :, hh * HEAD_DIM : (hh + 1) * HEAD_DIM] = (query_part * SCALE).astype(jnp.bfloat16)

    def give(src, dst, n, owner):
        @pl.when(owner == h)
        def _():
            pltpu.make_async_copy(src, dst, own_sem.at[n]).start()

        @pl.when(owner != h)
        def _():
            push(src, dst, out_send.at[n], out_recv.at[n], (s, owner))

    def give_query(j, r):
        col = pl.multiple_of((h * HEADS_KV + j) * PAIR, PAIR)
        for piece in range(2):
            half = slice(piece * (ROWS // 2), (piece + 1) * (ROWS // 2))
            give(dq_low.at[j, r, half], dq_hbm.at[half, pl.ds(col, PAIR)], 0, r)

    def give_kv(j, r):
        col = pl.multiple_of((h * HEADS_KV + j) * HEAD_DIM, HEAD_DIM)
        give(dkv_low.at[j, HALO + r, :, 0:HEAD_DIM], dk_hbm.at[:, pl.ds(col, HEAD_DIM)], 1, r)
        give(dkv_low.at[j, HALO + r, :, HEAD_DIM:], dv_hbm.at[:, pl.ds(col, HEAD_DIM)], 2, r)

    def rounded(j, b, extra=None):
        key_grad = dkv[j, b, :, 0:HEAD_DIM] * SCALE
        value_grad = dkv[j, b, :, HEAD_DIM:]
        if extra is not None:
            key_grad = key_grad + halo_in[j, extra, :, 0:HEAD_DIM].astype(jnp.float32)
            value_grad = value_grad + halo_in[j, extra, :, HEAD_DIM:].astype(jnp.float32)
        dkv_low[j, b, :, 0:HEAD_DIM] = key_grad.astype(jnp.bfloat16)
        dkv_low[j, b, :, HEAD_DIM:] = value_grad.astype(jnp.bfloat16)

    def finish_near(j):
        def one(n, carry):
            r = lax.rem(h + n, HALO)
            rounded(j, HALO + r)
            give_kv(j, r)
            return carry

        lax.fori_loop(0, HALO, one, 0)

    def finish_far(j):
        got(halo_in.at[j], back_recv.at[j])

        def one(n, carry):
            r = lax.rem(h + n, HALO)
            rounded(j, 2 * HALO + r, r)
            give_kv(j, HALO + r)
            return carry

        lax.fori_loop(0, HALO, one, 0)

    for j in range(HEADS_KV):
        got(kv.at[j, 0:HALO], halo_recv.at[j])
        for part in range(2):

            def one(n, carry):
                r = part * HALO + lax.rem(h + n, HALO)
                got(qg.at[j, r], qg_sem.at[j, r])
                unit(j, r)
                give_query(j, r)
                return carry

            lax.fori_loop(0, HALO, one, 0)
            if part == 0:

                def back(b, carry):
                    rounded(j, b)
                    push(dkv_low.at[j, b], halo_in.at[j, b], back_send.at[j], back_recv.at[j], before)
                    return carry

                lax.fori_loop(0, HALO, back, 0)
                if j > 0:
                    finish_far(j - 1)
        finish_near(j)
    finish_far(HEADS_KV - 1)

    for n in range(len(PEERS)):
        got(q_hbm.at[:, 0:1536], in_send.at[n])
    for j in range(HEADS_KV):
        got(kv.at[j, 0:HALO], halo_send.at[j])
        got(halo_in.at[j], back_send.at[j])
    for n, ref in enumerate((dq_hbm, dk_hbm, dv_hbm)):
        wide = ref.shape[1] // 8
        got(ref.at[:, 0:wide], own_sem.at[n])
        got(ref.at[:, 0 : 7 * wide], out_send.at[n])
        got(ref.at[:, 0 : 7 * wide], out_recv.at[n])


def local(queries, key_rows, value_rows, output_grad):
    anywhere = pl.BlockSpec(memory_space=pl.ANY)
    dma = pltpu.SemaphoreType.DMA
    blocks = 8 + HALO
    wide = SPAN * ROWS
    return pl.pallas_call(
        functools.partial(kernel, lax.axis_size("seq")),
        out_shape=[jax.ShapeDtypeStruct(a.shape, a.dtype) for a in (queries, key_rows, value_rows)],
        in_specs=[anywhere] * 4,
        out_specs=[anywhere] * 3,
        scratch_shapes=[
            pltpu.VMEM((HEADS_KV, 8, ROWS, 2 * PAIR), jnp.bfloat16),
            pltpu.VMEM((HEADS_KV, blocks, ROWS, 2 * HEAD_DIM), jnp.bfloat16),
            pltpu.VMEM((HEADS_KV, blocks, ROWS, 2 * HEAD_DIM), jnp.float32),
            pltpu.VMEM((HEADS_KV, blocks, ROWS, 2 * HEAD_DIM), jnp.bfloat16),
            pltpu.VMEM((HEADS_KV, HALO, ROWS, 2 * HEAD_DIM), jnp.bfloat16),
            pltpu.VMEM((HEADS_KV, 8, ROWS, PAIR), jnp.bfloat16),
            pltpu.VMEM((wide, ROWS), jnp.float32),
            pltpu.VMEM((wide, ROWS), jnp.float32),
            pltpu.VMEM((wide, ROWS), jnp.bfloat16),
            pltpu.VMEM((wide, ROWS), jnp.bfloat16),
            dma((HEADS_KV, 8)),
            dma((HEADS_KV, 8)),
            dma((len(PEERS),)),
            dma((HEADS_KV,)),
            dma((HEADS_KV,)),
            dma((HEADS_KV,)),
            dma((HEADS_KV,)),
            dma((3,)),
            dma((3,)),
            dma((3,)),
        ],
        compiler_params=pltpu.CompilerParams(
            collective_id=0, has_side_effects=True, vmem_limit_bytes=60 * 2**20
        ),
        name="window_grads",
    )(queries, key_rows, value_rows, output_grad)


def solution(mesh):
    placed = P(("seq", "head"), None)
    return jax.shard_map(
        local, mesh=mesh, in_specs=(placed,) * 4, out_specs=(placed,) * 3, check_vma=False
    )
```

time: 382 us -> 163 us (0.43)
  the two profiles are of different devices: /device:TPU:0 before, /device:TPU:6 now
where the time goes in v1:
time: 163 us
  Pallas kernels  157 us (96%)
  local copies, waits for them, and re-layouts  5.22 us (3%)
    pallas_call x1, Pallas kernels, local(): pl.pallas_call(functools.partial(kernel, lax.axis_size('seq')), out_shape...  157 us
    unnamed x7, local copies, waits for them, and re-layouts  5.22 us

profile of v1, /device:TPU:6, one launch (start us, length us, event | category | flops | bytes accessed | tf_op | source)
XLA Modules:
  0.0 163.2 jit_solution(13330230051542706678)
XLA Ops:
  0.6 157.3 %window_grads.1 = (bf16[256,4096]{1,0:T(8,128)(2,1)}, bf16[256,2048]{1,0:T(8,128)(2,1)}, bf16[256,2048]{1,0:T(8,128)(2,1)}) custom-call(bf16[256,4096]{1,0:T(8,128)(2,1)} %q_hbm.1, bf16[256,2048]{1,0:T(8,128)(2,1)} %k_hbm.1, bf16[256,2048]{1,0:T(8,128)(2,1)} %v_hbm.1, bf16[256,4096]{1,0:T(8,128)(2,1)} %g_hbm.1), custom_call_target="tpu_custom_call" | custom-call | tf_op jit(solution)/shard_map/window_grads/pallas_call | solution.py:291
  158.0 0.0 copy-start.1
  158.0 0.0 copy-start
  158.0 3.3 %copy.10 = bf16[256,4096]{1,0:T(8,128)(2,1)} copy(bf16[256,4096]{1,0:T(8,128)(2,1)} %get-tuple-element.6) | data formatting | bytes 4194304
  161.3 0.0 copy-done.1
  161.3 1.0 copy.11
  162.2 0.0 copy-done
  162.2 1.0 copy.12
Async XLA Ops:
  158.0 3.3 %copy-start.1 = (bf16[256,2048]{1,0:T(8,128)(2,1)S(1)}, bf16[256,2048]{1,0:T(8,128)(2,1)}, u32[]{:S(2)}) copy-start(bf16[256,2048]{1,0:T(8,128)(2,1)} %get-tuple-element.7) | copy-start | bytes 3145732
  158.0 4.3 %copy-start = (bf16[256,2048]{1,0:T(8,128)(2,1)S(1)}, bf16[256,2048]{1,0:T(8,128)(2,1)}, u32[]{:S(2)}) copy-start(bf16[256,2048]{1,0:T(8,128)(2,1)} %get-tuple-element.8) | copy-start | bytes 3145732

commit v2 on v1

v2 whole, which is shorter than its diff:
```python
import functools
import math

import jax
import jax.numpy as jnp
from jax import lax
from jax.experimental import pallas as pl
from jax.experimental.pallas import tpu as pltpu
from jax.sharding import PartitionSpec as P

HEAD_DIM = 128
WINDOW = 1024
GROUP = 2
SCALE = 168.0 ** (-0.5)
LOG2E = math.log2(math.e)
NEG = -1e30

ROWS = 256
HALO = WINDOW // ROWS
SPAN = HALO + 1
ALONG = 4
BLOCKS = 8
HEADS_KV = 4
PAIR = GROUP * HEAD_DIM
MESH = pl.DeviceIdType.MESH
STEPS = (2, 1, 3)


def fold(op, value):
    out = value[0:8]
    for begin in range(8, value.shape[0], 8):
        out = op(out, value[begin : begin + 8])
    return out


def kernel(
    seq_count,
    q_hbm,
    k_hbm,
    v_hbm,
    g_hbm,
    dq_hbm,
    dk_hbm,
    dv_hbm,
    qg,
    kv,
    dkv,
    dkv_low,
    back_in,
    part_in,
    dq_low,
    s_buf,
    g_buf,
    p_low,
    s_low,
    qg_sem,
    kv_sem,
    in_send,
    cross_send,
    cross_recv,
    halo_send,
    halo_recv,
    back_send,
    back_recv,
    part_send,
    part_recv,
    out_send,
    out_recv,
    own_sem,
):
    s, h = lax.axis_index("seq"), lax.axis_index("head")
    x, y = h // 2, lax.rem(h, 2)
    core = lax.rem(s, 2)
    mate = s + 1 - 2 * core
    other = lax.rem(s + 2 * core - 1 + seq_count, seq_count)
    others = [(other, x * 2 + half) for half in range(2)]
    peers = [lax.rem(x + dx, ALONG) * 2 + y for dx in STEPS]
    twin = (s, x * 2 + 1 - y)

    barrier = pltpu.get_barrier_semaphore()
    met = [(s, peer) for peer in peers] + [twin, (mate, h)] + others
    for device in met:
        pl.semaphore_signal(barrier, inc=1, device_id=device, device_id_type=MESH)
    pl.semaphore_wait(barrier, len(met))

    def push(src, dst, send, recv, device):
        pltpu.make_async_remote_copy(
            src_ref=src, dst_ref=dst, send_sem=send, recv_sem=recv, device_id=device, device_id_type=MESH
        ).start()

    def got(ref, sem):
        pltpu.make_async_copy(ref, ref, sem).wait()

    def kv_part(j, owner_x, part):
        col = pl.multiple_of((owner_x * HEADS_KV + j) * HEAD_DIM, HEAD_DIM)
        ref = (k_hbm, v_hbm)[part]
        return ref.at[:, pl.ds(col, HEAD_DIM)], kv.at[j, HALO + h, :, part * HEAD_DIM : (part + 1) * HEAD_DIM]

    def qg_part(j, owner_x, part, piece):
        col = pl.multiple_of((owner_x * HEADS_KV + j) * PAIR, PAIR)
        half = slice(piece * (ROWS // 2), (piece + 1) * (ROWS // 2))
        ref = (q_hbm, g_hbm)[part]
        return ref.at[half, pl.ds(col, PAIR)], qg.at[j, x, half, part * PAIR : (part + 1) * PAIR]

    def push_kv(j):
        for part in range(2):
            for n, peer in enumerate(peers):
                src, dst = kv_part(j, peer // 2, part)
                push(src, dst, in_send.at[n], kv_sem.at[j, x], (s, peer))

    def push_qg(j):
        for piece in range(2):
            for part in range(2):
                for n, peer in enumerate(peers):
                    src, dst = qg_part(j, peer // 2, part, piece)
                    push(src, dst, in_send.at[n], qg_sem.at[j, x], (s, peer))

    push_kv(0)
    push_kv(1)
    push_qg(0)
    push_kv(2)
    push_qg(1)
    push_kv(3)
    push_qg(2)
    push_qg(3)

    def take_own(j, carry):
        for part in range(2):
            src, dst = kv_part(j, x, part)
            pltpu.make_async_copy(src, dst, kv_sem.at[j, x]).start()
            for piece in range(2):
                src, dst = qg_part(j, x, part, piece)
                pltpu.make_async_copy(src, dst, qg_sem.at[j, x]).start()
        return carry

    lax.fori_loop(0, HEADS_KV, take_own, 0)

    def clear(b, carry):
        for j in range(HEADS_KV):
            dkv[j, b] = jnp.zeros((ROWS, 2 * HEAD_DIM), jnp.float32)
        return carry

    lax.fori_loop(0, BLOCKS + HALO, clear, 0)

    def spread_kv(j):
        for i in range(ALONG):
            got(kv.at[j, HALO + 2 * i + y], kv_sem.at[j, i])
        for i in range(ALONG):
            block = kv.at[j, HALO + 2 * i + y]
            push(block, block, cross_send.at[j], cross_recv.at[j], twin)

        @pl.when(core == 1)
        def _():
            for i in range(2):
                for device in others:
                    push(
                        kv.at[j, BLOCKS + 2 * i + y],
                        kv.at[j, 2 * i + y],
                        halo_send.at[j],
                        halo_recv.at[j],
                        device,
                    )

    def halo_on_chip(j):
        got(kv.at[j, 0:ALONG], cross_recv.at[j])

        @pl.when(core == 0)
        def _():
            for b in range(HALO):
                push(kv.at[j, BLOCKS + b], kv.at[j, b], halo_send.at[j], halo_recv.at[j], (mate, h))

    key_row = lax.broadcasted_iota(jnp.int32, (ROWS, ROWS), 0)
    query_col = lax.broadcasted_iota(jnp.int32, (ROWS, ROWS), 1)

    def unit(j, i):
        r = 2 * i + y
        keys = kv[j, pl.ds(r, SPAN), :, 0:HEAD_DIM].reshape(SPAN * ROWS, HEAD_DIM)
        values = kv[j, pl.ds(r, SPAN), :, HEAD_DIM:].reshape(SPAN * ROWS, HEAD_DIM)
        for hh in range(GROUP):
            query = qg[j, i, :, hh * HEAD_DIM : (hh + 1) * HEAD_DIM]
            grad = qg[j, i, :, PAIR + hh * HEAD_DIM : PAIR + (hh + 1) * HEAD_DIM]
            nt = (((1,), (1,)), ((), ()))
            s_buf[...] = lax.dot_general(keys, query, nt, preferred_element_type=jnp.float32)
            g_buf[...] = lax.dot_general(values, grad, nt, preferred_element_type=jnp.float32)
            peak = jnp.full((8, ROWS), NEG, jnp.float32)
            for c in range(SPAN):
                part = s_buf[c * ROWS : (c + 1) * ROWS]
                if c < HALO:
                    inside = (s > 0) | (r + c >= HALO)
                    if c == 0:
                        part = jnp.where((key_row > query_col) & inside, part, NEG)
                    else:
                        part = jnp.where(inside, part, NEG)
                else:
                    part = jnp.where(key_row <= query_col, part, NEG)
                s_buf[c * ROWS : (c + 1) * ROWS] = part
                peak = jnp.maximum(peak, fold(jnp.maximum, part))
            peak = jnp.max(peak, axis=0, keepdims=True)
            total = jnp.zeros((8, ROWS), jnp.float32)
            centre = jnp.zeros((8, ROWS), jnp.float32)
            step = 64
            for begin in range(0, SPAN * ROWS, step):
                at = slice(begin, begin + step)
                raised = jnp.exp2((s_buf[at] - peak) * (SCALE * LOG2E))
                s_buf[at] = raised
                total = total + fold(jnp.add, raised)
                centre = centre + fold(jnp.add, raised * g_buf[at])
            scale = 1.0 / jnp.sum(total, axis=0, keepdims=True)
            centre = jnp.sum(centre, axis=0, keepdims=True) * scale
            for begin in range(0, SPAN * ROWS, step):
                at = slice(begin, begin + step)
                prob = s_buf[at] * scale
                p_low[at] = prob.astype(jnp.bfloat16)
                s_low[at] = (prob * (g_buf[at] - centre)).astype(jnp.bfloat16)
            nn = (((1,), (0,)), ((), ()))
            key_part = lax.dot_general(s_low[...], query, nn, preferred_element_type=jnp.float32)
            value_part = lax.dot_general(p_low[...], grad, nn, preferred_element_type=jnp.float32)
            for c in range(SPAN):
                at = slice(c * ROWS, (c + 1) * ROWS)
                dkv[j, r + c, :, 0:HEAD_DIM] += key_part[at]
                dkv[j, r + c, :, HEAD_DIM:] += value_part[at]
            query_part = lax.dot_general(
                s_low[...], keys, (((0,), (0,)), ((), ())), preferred_element_type=jnp.float32
            )
            dq_low[j, i, :, hh * HEAD_DIM : (hh + 1) * HEAD_DIM] = (query_part * SCALE).astype(jnp.bfloat16)

    def rounded(j, b, extras=()):
        key_grad = dkv[j, b, :, 0:HEAD_DIM] * SCALE
        value_grad = dkv[j, b, :, HEAD_DIM:]
        for extra in extras:
            key_grad = key_grad + extra[:, 0:HEAD_DIM].astype(jnp.float32)
            value_grad = value_grad + extra[:, HEAD_DIM:].astype(jnp.float32)
        dkv_low[j, b, :, 0:HEAD_DIM] = key_grad.astype(jnp.bfloat16)
        dkv_low[j, b, :, HEAD_DIM:] = value_grad.astype(jnp.bfloat16)

    def give_back(j):
        def one(b, carry):
            rounded(j, b)
            block = dkv_low.at[j, b]

            @pl.when(core == 1)
            def _():
                push(block, back_in.at[j, b], back_send.at[j], back_recv.at[j], (mate, h))

            @pl.when(core == 0)
            def _():
                slot = 2 * y + b // 2
                to = (other, x * 2 + lax.rem(b, 2))
                push(block, back_in.at[j, slot], back_send.at[j], back_recv.at[j], to)

            return carry

        lax.fori_loop(0, HALO, one, 0)

    def give_twin(j):
        def send(i, extras=()):
            b = HALO + 2 * i + 1 - y
            rounded(j, b, extras)
            push(dkv_low.at[j, b], part_in.at[j, i], part_send.at[j], part_recv.at[j], twin)

        def near(i, carry):
            send(i)
            return carry

        lax.fori_loop(0, 2, near, 0)
        got(back_in.at[j], back_recv.at[j])

        def far(i, carry):
            @pl.when(core == 0)
            def _():
                send(i, (back_in[j, 2 * i + 1 - y - HALO],))

            @pl.when(core == 1)
            def _():
                send(i)

            return carry

        lax.fori_loop(2, ALONG, far, 0)

    def give(src, dst, n, owner_x):
        @pl.when(owner_x == x)
        def _():
            pltpu.make_async_copy(src, dst, own_sem.at[n]).start()

        @pl.when(owner_x != x)
        def _():
            push(src, dst, out_send.at[n], out_recv.at[n], (s, owner_x * 2 + y))

    def give_query(j):
        col = pl.multiple_of((x * HEADS_KV + j) * PAIR, PAIR)
        for piece in range(2):
            half = slice(piece * (ROWS // 2), (piece + 1) * (ROWS // 2))
            for dx in STEPS + (0,):
                i = lax.rem(x + dx, ALONG)
                give(dq_low.at[j, i, half], dq_hbm.at[half, pl.ds(col, PAIR)], 0, i)

    def give_kv(j):
        got(part_in.at[j], part_recv.at[j])

        def one(i, carry):
            b = HALO + 2 * i + y

            @pl.when(i < 2)
            def _():
                rounded(j, b, (part_in[j, i],))

            @pl.when((i >= 2) & (core == 0))
            def _():
                rounded(j, b, (part_in[j, i], back_in[j, lax.rem(2 * i + y, HALO)]))

            @pl.when((i >= 2) & (core == 1))
            def _():
                slot = lax.rem(i, 2)
                rounded(j, b, (part_in[j, i], back_in[j, slot], back_in[j, 2 + slot]))

            return carry

        lax.fori_loop(0, ALONG, one, 0)
        col = pl.multiple_of((x * HEADS_KV + j) * HEAD_DIM, HEAD_DIM)
        for n, ref in ((1, dk_hbm), (2, dv_hbm)):
            for dx in STEPS + (0,):
                i = lax.rem(x + dx, ALONG)
                at = slice((n - 1) * HEAD_DIM, n * HEAD_DIM)
                give(dkv_low.at[j, HALO + 2 * i + y, :, at], ref.at[:, pl.ds(col, HEAD_DIM)], n, i)

    spread_kv(0)
    spread_kv(1)
    halo_on_chip(0)

    def head(j, carry):
        got(kv.at[j, 0:HALO], halo_recv.at[j])
        for i in range(ALONG):
            got(qg.at[j, i], qg_sem.at[j, i])

        def half(part, carry):
            def one(n, carry):
                unit(j, 2 * part + lax.rem(x + n, 2))
                return carry

            lax.fori_loop(0, 2, one, 0)

            @pl.when(part == 0)
            def _():
                give_back(j)

                @pl.when(j + 2 < HEADS_KV)
                def _():
                    spread_kv(j + 2)

                @pl.when(j + 1 < HEADS_KV)
                def _():
                    halo_on_chip(j + 1)

                @pl.when(j >= 1)
                def _():
                    give_kv(j - 1)

            return carry

        lax.fori_loop(0, 2, half, 0)
        give_query(j)
        give_twin(j)
        return carry

    lax.fori_loop(0, HEADS_KV, head, 0)
    give_kv(HEADS_KV - 1)

    for n in range(len(STEPS)):
        got(q_hbm.at[:, 0:3072], in_send.at[n])
    for j in range(HEADS_KV):
        for sem in (cross_send, halo_send, back_send, part_send):
            got(back_in.at[j], sem.at[j])
    for n, ref in enumerate((dq_hbm, dk_hbm, dv_hbm)):
        wide = ref.shape[1] // ALONG
        got(ref.at[:, 0:wide], own_sem.at[n])
        got(ref.at[:, 0 : 3 * wide], out_send.at[n])
        got(ref.at[:, 0 : 3 * wide], out_recv.at[n])


def local(queries, key_rows, value_rows, output_grad):
    anywhere = pl.BlockSpec(memory_space=pl.ANY)
    dma = pltpu.SemaphoreType.DMA
    blocks = BLOCKS + HALO
    wide = SPAN * ROWS
    return pl.pallas_call(
        functools.partial(kernel, lax.axis_size("seq")),
        out_shape=[jax.ShapeDtypeStruct(a.shape, a.dtype) for a in (queries, key_rows, value_rows)],
        in_specs=[anywhere] * 4,
        out_specs=[anywhere] * 3,
        scratch_shapes=[
            pltpu.VMEM((HEADS_KV, ALONG, ROWS, 2 * PAIR), jnp.bfloat16),
            pltpu.VMEM((HEADS_KV, blocks, ROWS, 2 * HEAD_DIM), jnp.bfloat16),
            pltpu.VMEM((HEADS_KV, blocks, ROWS, 2 * HEAD_DIM), jnp.float32),
            pltpu.VMEM((HEADS_KV, blocks, ROWS, 2 * HEAD_DIM), jnp.bfloat16),
            pltpu.VMEM((HEADS_KV, HALO, ROWS, 2 * HEAD_DIM), jnp.bfloat16),
            pltpu.VMEM((HEADS_KV, ALONG, ROWS, 2 * HEAD_DIM), jnp.bfloat16),
            pltpu.VMEM((HEADS_KV, ALONG, ROWS, PAIR), jnp.bfloat16),
            pltpu.VMEM((wide, ROWS), jnp.float32),
            pltpu.VMEM((wide, ROWS), jnp.float32),
            pltpu.VMEM((wide, ROWS), jnp.bfloat16),
            pltpu.VMEM((wide, ROWS), jnp.bfloat16),
            dma((HEADS_KV, ALONG)),
            dma((HEADS_KV, ALONG)),
            dma((len(STEPS),)),
            *[dma((HEADS_KV,)) for _ in range(8)],
            dma((3,)),
            dma((3,)),
            dma((3,)),
        ],
        compiler_params=pltpu.CompilerParams(
            collective_id=0, has_side_effects=True, vmem_limit_bytes=60 * 2**20
        ),
        name="window_grads",
    )(queries, key_rows, value_rows, output_grad)


def solution(mesh):
    placed = P(("seq", "head"), None)
    return jax.shard_map(
        local, mesh=mesh, in_specs=(placed,) * 4, out_specs=(placed,) * 3, check_vma=False
    )
```

time: 163 us -> 150 us (0.920)
  the two profiles are of different devices: /device:TPU:6 before, /device:TPU:0 now
where the time goes in v2:
time: 150 us
  Pallas kernels  144 us (96%)
  local copies, waits for them, and re-layouts  5.22 us (3%)
    pallas_call x1, Pallas kernels, local(): pl.pallas_call(functools.partial(kernel, lax.axis_size('seq')), out_shape...  144 us
    unnamed x7, local copies, waits for them, and re-layouts  5.22 us

profile of v2, /device:TPU:0, one launch (start us, length us, event | category | flops | bytes accessed | tf_op | source)
XLA Modules:
  0.0 150.0 jit_solution(17556350470731124707)
XLA Ops:
  0.6 144.1 %window_grads.1 = (bf16[256,4096]{1,0:T(8,128)(2,1)}, bf16[256,2048]{1,0:T(8,128)(2,1)}, bf16[256,2048]{1,0:T(8,128)(2,1)}) custom-call(bf16[256,4096]{1,0:T(8,128)(2,1)} %q_hbm.1, bf16[256,2048]{1,0:T(8,128)(2,1)} %k_hbm.1, bf16[256,2048]{1,0:T(8,128)(2,1)} %v_hbm.1, bf16[256,4096]{1,0:T(8,128)(2,1)} %g_hbm.1), custom_call_target="tpu_custom_call" | custom-call | tf_op jit(solution)/shard_map/window_grads/pallas_call | solution.py:386
  144.8 0.0 copy-start.1
  144.8 0.0 copy-start
  144.8 3.3 %copy.10 = bf16[256,4096]{1,0:T(8,128)(2,1)} copy(bf16[256,4096]{1,0:T(8,128)(2,1)} %get-tuple-element.6) | data formatting | bytes 4194304
  148.1 0.0 copy-done.1
  148.1 1.0 copy.11
  149.0 0.0 copy-done
  149.0 1.0 copy.12
Async XLA Ops:
  144.8 3.3 %copy-start.1 = (bf16[256,2048]{1,0:T(8,128)(2,1)S(1)}, bf16[256,2048]{1,0:T(8,128)(2,1)}, u32[]{:S(2)}) copy-start(bf16[256,2048]{1,0:T(8,128)(2,1)} %get-tuple-element.7) | copy-start | bytes 3145732
  144.8 4.3 %copy-start = (bf16[256,2048]{1,0:T(8,128)(2,1)S(1)}, bf16[256,2048]{1,0:T(8,128)(2,1)}, u32[]{:S(2)}) copy-start(bf16[256,2048]{1,0:T(8,128)(2,1)} %get-tuple-element.8) | copy-start | bytes 3145732

commit v3 on v2

--- a/solution.py
+++ b/solution.py
@@ -91,6 +91,18 @@
     def got(ref, sem):
         pltpu.make_async_copy(ref, ref, sem).wait()
 
+    def got_blocks(ref, sem, fewer):
+        @pl.when(fewer)
+        def _():
+            got(ref.at[1:4], sem)
+
+        @pl.when(jnp.logical_not(fewer))
+        def _():
+            got(ref.at[0:4], sem)
+
+    def cross_has(i, half):
+        return (i < ALONG - 1) | (half == 0) | (core == 0)
+
     def kv_part(j, owner_x, part):
         col = pl.multiple_of((owner_x * HEADS_KV + j) * HEAD_DIM, HEAD_DIM)
         ref = (k_hbm, v_hbm)[part]
@@ -116,6 +128,14 @@
                     push(src, dst, in_send.at[n], qg_sem.at[j, x], (s, peer))
 
     push_kv(0)
+    for j in range(HEADS_KV):
+
+        @pl.when(cross_has(x, y))
+        def _(j=j):
+            for part in range(2):
+                src, dst = kv_part(j, x, part)
+                push(src, dst, cross_send.at[j], cross_recv.at[j], twin)
+
     push_kv(1)
     push_qg(0)
     push_kv(2)
@@ -145,24 +165,30 @@
     def spread_kv(j):
         for i in range(ALONG):
             got(kv.at[j, HALO + 2 * i + y], kv_sem.at[j, i])
-        for i in range(ALONG):
-            block = kv.at[j, HALO + 2 * i + y]
-            push(block, block, cross_send.at[j], cross_recv.at[j], twin)
+        for dx in STEPS:
+            i = lax.rem(x + dx, ALONG)
+
+            @pl.when(cross_has(i, y))
+            def _(i=i):
+                block = kv.at[j, HALO + 2 * i + y]
+                push(block, block, cross_send.at[j], cross_recv.at[j], twin)
+
+        def send_halo(i, half):
+            src, dst = kv.at[j, BLOCKS + 2 * i + y], kv.at[j, 2 * i + y]
+            push(src, dst, halo_send.at[j], halo_recv.at[j], others[half])
 
         @pl.when(core == 1)
         def _():
             for i in range(2):
-                for device in others:
-                    push(
-                        kv.at[j, BLOCKS + 2 * i + y],
-                        kv.at[j, 2 * i + y],
-                        halo_send.at[j],
-                        halo_recv.at[j],
-                        device,
-                    )
+                send_halo(i, 0)
+            send_halo(1, 1)
+
+            @pl.when(y == 1)
+            def _():
+                send_halo(0, 1)
 
     def halo_on_chip(j):
-        got(kv.at[j, 0:ALONG], cross_recv.at[j])
+        got_blocks(kv.at[j], cross_recv.at[j], (core == 1) & (y == 0))
 
         @pl.when(core == 0)
         def _():
@@ -242,7 +268,7 @@
             def _():
                 push(block, back_in.at[j, b], back_send.at[j], back_recv.at[j], (mate, h))
 
-            @pl.when(core == 0)
+            @pl.when((core == 0) & (b >= y))
             def _():
                 slot = 2 * y + b // 2
                 to = (other, x * 2 + lax.rem(b, 2))
@@ -253,30 +279,27 @@
         lax.fori_loop(0, HALO, one, 0)
 
     def give_twin(j):
-        def send(i, extras=()):
+        got_blocks(back_in.at[j], back_recv.at[j], (core == 1) & (y == 0))
+
+        def one(n, carry):
+            i = lax.rem(x + jnp.where(n == 0, 2, jnp.where(n == 1, 1, jnp.where(n == 2, 3, 0))), ALONG)
             b = HALO + 2 * i + 1 - y
-            rounded(j, b, extras)
-            push(dkv_low.at[j, b], part_in.at[j, i], part_send.at[j], part_recv.at[j], twin)
-
-        def near(i, carry):
-            send(i)
+
+            @pl.when((core == 0) & (i >= 2))
+            def _():
+                rounded(j, b, (back_in[j, lax.rem(2 * i + 1 - y, HALO)],))
+
+            @pl.when((core == 1) | (i < 2))
+            def _():
+                rounded(j, b)
+
+            @pl.when(cross_has(i, 1 - y))
+            def _():
+                push(dkv_low.at[j, b], part_in.at[j, i], part_send.at[j], part_recv.at[j, i], twin)
+
             return carry
 
-        lax.fori_loop(0, 2, near, 0)
-        got(back_in.at[j], back_recv.at[j])
-
-        def far(i, carry):
-            @pl.when(core == 0)
-            def _():
-                send(i, (back_in[j, 2 * i + 1 - y - HALO],))
-
-            @pl.when(core == 1)
-            def _():
-                send(i)
-
-            return carry
-
-        lax.fori_loop(2, ALONG, far, 0)
+        lax.fori_loop(0, ALONG, one, 0)
 
     def give(src, dst, n, owner_x):
         @pl.when(owner_x == x)
@@ -296,10 +319,16 @@
                 give(dq_low.at[j, i, half], dq_hbm.at[half, pl.ds(col, PAIR)], 0, i)
 
     def give_kv(j):
-        got(part_in.at[j], part_recv.at[j])
-
-        def one(i, carry):
+        col = pl.multiple_of((x * HEADS_KV + j) * HEAD_DIM, HEAD_DIM)
+
+        def one(n, carry):
+            i = lax.rem(x + jnp.where(n == 0, 2, jnp.where(n == 1, 1, jnp.where(n == 2, 3, 0))), ALONG)
             b = HALO + 2 * i + y
+            slot = lax.rem(i, 2)
+
+            @pl.when(cross_has(i, y))
+            def _():
+                got(part_in.at[j, i], part_recv.at[j, i])
 
             @pl.when(i < 2)
             def _():
@@ -309,27 +338,34 @@
             def _():
                 rounded(j, b, (part_in[j, i], back_in[j, lax.rem(2 * i + y, HALO)]))
 
-            @pl.when((i >= 2) & (core == 1))
-            def _():
-                slot = lax.rem(i, 2)
+            @pl.when((i == 2) & (core == 1) & (y == 0))
+            def _():
+                rounded(j, b, (part_in[j, i], back_in[j, slot]))
+
+            @pl.when((i == 2) & (core == 1) & (y == 1))
+            def _():
                 rounded(j, b, (part_in[j, i], back_in[j, slot], back_in[j, 2 + slot]))
 
+            @pl.when((i == 3) & (core == 1) & (y == 0))
+            def _():
+                rounded(j, b, (part_in[j, i], back_in[j, slot], back_in[j, 2 + slot]))
+
+            @pl.when((i == 3) & (core == 1) & (y == 1))
+            def _():
+                rounded(j, b, (back_in[j, slot], back_in[j, 2 + slot]))
+
+            give(dkv_low.at[j, b, :, 0:HEAD_DIM], dk_hbm.at[:, pl.ds(col, HEAD_DIM)], 1, i)
+            give(dkv_low.at[j, b, :, HEAD_DIM:], dv_hbm.at[:, pl.ds(col, HEAD_DIM)], 2, i)
             return carry
 
         lax.fori_loop(0, ALONG, one, 0)
-        col = pl.multiple_of((x * HEADS_KV + j) * HEAD_DIM, HEAD_DIM)
-        for n, ref in ((1, dk_hbm), (2, dv_hbm)):
-            for dx in STEPS + (0,):
-                i = lax.rem(x + dx, ALONG)
-                at = slice((n - 1) * HEAD_DIM, n * HEAD_DIM)
-                give(dkv_low.at[j, HALO + 2 * i + y, :, at], ref.at[:, pl.ds(col, HEAD_DIM)], n, i)
 
     spread_kv(0)
     spread_kv(1)
     halo_on_chip(0)
 
     def head(j, carry):
-        got(kv.at[j, 0:HALO], halo_recv.at[j])
+        got_blocks(kv.at[j], halo_recv.at[j], (core == 0) & (y == 1))
         for i in range(ALONG):
             got(qg.at[j, i], qg_sem.at[j, i])
 
@@ -352,15 +388,16 @@
                 def _():
                     halo_on_chip(j + 1)
 
-                @pl.when(j >= 1)
-                def _():
-                    give_kv(j - 1)
-
             return carry
 
         lax.fori_loop(0, 2, half, 0)
         give_query(j)
         give_twin(j)
+
+        @pl.when(j >= 1)
+        def _():
+            give_kv(j - 1)
+
         return carry
 
     lax.fori_loop(0, HEADS_KV, head, 0)
@@ -369,8 +406,10 @@
     for n in range(len(STEPS)):
         got(q_hbm.at[:, 0:3072], in_send.at[n])
     for j in range(HEADS_KV):
-        for sem in (cross_send, halo_send, back_send, part_send):
-            got(back_in.at[j], sem.at[j])
+        got_blocks(back_in.at[j], cross_send.at[j], (core == 1) & (y == 1))
+        got_blocks(back_in.at[j], halo_send.at[j], (core == 1) & (y == 0))
+        got_blocks(back_in.at[j], back_send.at[j], (core == 0) & (y == 1))
+        got_blocks(back_in.at[j], part_send.at[j], (core == 1) & (y == 0))
     for n, ref in enumerate((dq_hbm, dk_hbm, dv_hbm)):
         wide = ref.shape[1] // ALONG
         got(ref.at[:, 0:wide], own_sem.at[n])
@@ -403,7 +442,8 @@
             dma((HEADS_KV, ALONG)),
             dma((HEADS_KV, ALONG)),
             dma((len(STEPS),)),
-            *[dma((HEADS_KV,)) for _ in range(8)],
+            *[dma((HEADS_KV,)) for _ in range(7)],
+            dma((HEADS_KV, ALONG)),
             dma((3,)),
             dma((3,)),
             dma((3,)),

time: 150 us -> 131 us (0.87); the launches traced: 150 us -> 129 us
  Pallas kernels: 144 us -> 123 us
    pallas_call x1, Pallas kernels: 144 us -> 123 us  [local(): pl.pallas_call(functools.partial(kernel, lax.axis_size('seq')), out_shape...]
where the time goes in v3:
time: 131 us; the launch traced here: 129 us
  Pallas kernels  123 us (94%)
  local copies, waits for them, and re-layouts  5.22 us (4%)
    pallas_call x1, Pallas kernels, local(): pl.pallas_call(functools.partial(kernel, lax.axis_size('seq')), out_shape...  123 us
    unnamed x7, local copies, waits for them, and re-layouts  5.22 us

profile of v3, /device:TPU:0, one launch (start us, length us, event | category | flops | bytes accessed | tf_op | source)
XLA Modules:
  0.0 128.9 jit_solution(3484543505003606045)
XLA Ops:
  0.6 123.1 %window_grads.1 = (bf16[256,4096]{1,0:T(8,128)(2,1)}, bf16[256,2048]{1,0:T(8,128)(2,1)}, bf16[256,2048]{1,0:T(8,128)(2,1)}) custom-call(bf16[256,4096]{1,0:T(8,128)(2,1)} %q_hbm.1, bf16[256,2048]{1,0:T(8,128)(2,1)} %k_hbm.1, bf16[256,2048]{1,0:T(8,128)(2,1)} %v_hbm.1, bf16[256,4096]{1,0:T(8,128)(2,1)} %g_hbm.1), custom_call_target="tpu_custom_call" | custom-call | tf_op jit(solution)/shard_map/window_grads/pallas_call | solution.py:425
  123.7 0.0 copy-start.1
  123.7 0.0 copy-start
  123.7 3.3 %copy.10 = bf16[256,4096]{1,0:T(8,128)(2,1)} copy(bf16[256,4096]{1,0:T(8,128)(2,1)} %get-tuple-element.6) | data formatting | bytes 4194304
  127.0 0.0 copy-done.1
  127.0 1.0 copy.11
  128.0 0.0 copy-done
  128.0 1.0 copy.12
Async XLA Ops:
  123.7 3.3 %copy-start.1 = (bf16[256,2048]{1,0:T(8,128)(2,1)S(1)}, bf16[256,2048]{1,0:T(8,128)(2,1)}, u32[]{:S(2)}) copy-start(bf16[256,2048]{1,0:T(8,128)(2,1)} %get-tuple-element.7) | copy-start | bytes 3145732
  123.7 4.3 %copy-start = (bf16[256,2048]{1,0:T(8,128)(2,1)S(1)}, bf16[256,2048]{1,0:T(8,128)(2,1)}, u32[]{:S(2)}) copy-start(bf16[256,2048]{1,0:T(8,128)(2,1)} %get-tuple-element.8) | copy-start | bytes 3145732

commit v4 on v3

--- a/solution.py
+++ b/solution.py
@@ -417,14 +417,28 @@
         got(ref.at[:, 0 : 3 * wide], out_recv.at[n])
 
 
+def write_out(*refs):
+    sems = refs[-1]
+    copies = []
+    for n in range(3):
+        rows = refs[n].shape[0] // 4
+        for m in range(4):
+            at = pl.ds(m * rows, rows)
+            copies.append(pltpu.make_async_copy(refs[n].at[at], refs[3 + n].at[at], sems.at[n, m]))
+    for copy in copies:
+        copy.start()
+    for copy in copies:
+        copy.wait()
+
+
 def local(queries, key_rows, value_rows, output_grad):
     anywhere = pl.BlockSpec(memory_space=pl.ANY)
     dma = pltpu.SemaphoreType.DMA
     blocks = BLOCKS + HALO
     wide = SPAN * ROWS
-    return pl.pallas_call(
+    held = pl.pallas_call(
         functools.partial(kernel, lax.axis_size("seq")),
-        out_shape=[jax.ShapeDtypeStruct(a.shape, a.dtype) for a in (queries, key_rows, value_rows)],
+        out_shape=[pltpu.VMEM(a.shape, a.dtype) for a in (queries, key_rows, value_rows)],
         in_specs=[anywhere] * 4,
         out_specs=[anywhere] * 3,
         scratch_shapes=[
@@ -449,10 +463,20 @@
             dma((3,)),
         ],
         compiler_params=pltpu.CompilerParams(
-            collective_id=0, has_side_effects=True, vmem_limit_bytes=60 * 2**20
+            collective_id=0, has_side_effects=True, vmem_limit_bytes=52 * 2**20
         ),
         name="window_grads",
     )(queries, key_rows, value_rows, output_grad)
+    held = [pltpu.with_memory_space_constraint(a, pltpu.VMEM) for a in held]
+    return pl.pallas_call(
+        write_out,
+        out_shape=[jax.ShapeDtypeStruct(a.shape, a.dtype) for a in (queries, key_rows, value_rows)],
+        in_specs=[anywhere] * 3,
+        out_specs=[anywhere] * 3,
+        scratch_shapes=[dma((3, 4))],
+        compiler_params=pltpu.CompilerParams(vmem_limit_bytes=4 * 2**20),
+        name="write_out",
+    )(*held)
 
 
 def solution(mesh):

time: 131 us -> 128 us (0.977)
  local copies, waits for them, and re-layouts: 5.22 us -> 0 us
  Pallas kernels: 123 us -> 125 us
    unnamed x7 -> x0, local copies, waits for them, and re-layouts: 5.22 us -> none
    pallas_call x0 -> x1, Pallas kernels: none -> 2.1 us  [local(): pl.pallas_call(write_out, out_shape=[jax.ShapeDtypeStruct(a.shape, a.dtyp...]
where the time goes in v4:
time: 128 us; the launch traced here: 126 us
  Pallas kernels  125 us (98%)
    pallas_call x1, Pallas kernels, local(): pl.pallas_call(functools.partial(kernel, lax.axis_size('seq')), out_shape...  123 us

profile of v4, /device:TPU:0, one launch (start us, length us, event | category | flops | bytes accessed | tf_op | source)
XLA Modules:
  0.0 125.6 jit_solution(13548012560233108502)
XLA Ops:
  0.6 122.9 %window_grads.1 = (bf16[256,4096]{1,0:T(8,128)(2,1)S(1)}, bf16[256,2048]{1,0:T(8,128)(2,1)S(1)}, bf16[256,2048]{1,0:T(8,128)(2,1)S(1)}) custom-call(bf16[256,4096]{1,0:T(8,128)(2,1)} %q_hbm.1, bf16[256,2048]{1,0:T(8,128)(2,1)} %k_hbm.1, bf16[256,2048]{1,0:T(8,128)(2,1)} %v_hbm.1, bf16[256,4096]{1,0:T(8,128)(2,1)} %g_hbm.1), custom_call_target="tpu_custom_call" | custom-call | tf_op jit(solution)/shard_map/window_grads/pallas_call | solution.py:439
  123.5 2.1 %write_out.1 = (bf16[256,4096]{1,0:T(8,128)(2,1)}, bf16[256,2048]{1,0:T(8,128)(2,1)}, bf16[256,2048]{1,0:T(8,128)(2,1)}) custom-call(bf16[256,4096]{1,0:T(8,128)(2,1)S(1)} %get-tuple-element.6.refs_0_, bf16[256,2048]{1,0:T(8,128)(2,1)S(1)} %get-tuple-element.7.refs_1_, bf16[256,2048]{1,0:T(8,128)(2,1)S(1)} %get-tuple-element.8.refs_2_), custom_call_target="tpu_custom_call" | custom-call | tf_op jit(solution)/shard_map/write_out/pallas_call | solution.py:471

commit v5 on v4

--- a/solution.py
+++ b/solution.py
@@ -49,8 +49,8 @@
     back_in,
     part_in,
     dq_low,
-    s_buf,
-    g_buf,
+    s_two,
+    g_two,
     p_low,
     s_low,
     qg_sem,
@@ -121,11 +121,12 @@
                 push(src, dst, in_send.at[n], kv_sem.at[j, x], (s, peer))
 
     def push_qg(j):
-        for piece in range(2):
-            for part in range(2):
-                for n, peer in enumerate(peers):
-                    src, dst = qg_part(j, peer // 2, part, piece)
-                    push(src, dst, in_send.at[n], qg_sem.at[j, x], (s, peer))
+        for group in ((0,), (1, 2)):
+            for piece in range(2):
+                for part in range(2):
+                    for n in group:
+                        src, dst = qg_part(j, peers[n] // 2, part, piece)
+                        push(src, dst, in_send.at[n], qg_sem.at[j, x], (s, peers[n]))
 
     push_kv(0)
     for j in range(HEADS_KV):
@@ -198,36 +199,41 @@
     key_row = lax.broadcasted_iota(jnp.int32, (ROWS, ROWS), 0)
     query_col = lax.broadcasted_iota(jnp.int32, (ROWS, ROWS), 1)
 
+    nt = (((1,), (1,)), ((), ()))
+    nn = (((1,), (0,)), ((), ()))
+    tn = (((0,), (0,)), ((), ()))
+
     def unit(j, i):
         r = 2 * i + y
         keys = kv[j, pl.ds(r, SPAN), :, 0:HEAD_DIM].reshape(SPAN * ROWS, HEAD_DIM)
         values = kv[j, pl.ds(r, SPAN), :, HEAD_DIM:].reshape(SPAN * ROWS, HEAD_DIM)
+        inside = [(s > 0) | (r + c >= HALO) for c in range(HALO)]
         for hh in range(GROUP):
             query = qg[j, i, :, hh * HEAD_DIM : (hh + 1) * HEAD_DIM]
             grad = qg[j, i, :, PAIR + hh * HEAD_DIM : PAIR + (hh + 1) * HEAD_DIM]
-            nt = (((1,), (1,)), ((), ()))
-            s_buf[...] = lax.dot_general(keys, query, nt, preferred_element_type=jnp.float32)
-            g_buf[...] = lax.dot_general(values, grad, nt, preferred_element_type=jnp.float32)
+            s_two[hh] = lax.dot_general(keys, query, nt, preferred_element_type=jnp.float32)
+            g_two[hh] = lax.dot_general(values, grad, nt, preferred_element_type=jnp.float32)
+        for hh in range(GROUP):
+            cols = slice(hh * ROWS, (hh + 1) * ROWS)
+            s_buf, g_buf = s_two.at[hh], g_two.at[hh]
+
             peak = jnp.full((8, ROWS), NEG, jnp.float32)
             for c in range(SPAN):
                 part = s_buf[c * ROWS : (c + 1) * ROWS]
-                if c < HALO:
-                    inside = (s > 0) | (r + c >= HALO)
-                    if c == 0:
-                        part = jnp.where((key_row > query_col) & inside, part, NEG)
-                    else:
-                        part = jnp.where(inside, part, NEG)
-                else:
-                    part = jnp.where(key_row <= query_col, part, NEG)
-                s_buf[c * ROWS : (c + 1) * ROWS] = part
-                peak = jnp.maximum(peak, fold(jnp.maximum, part))
+                if c in (0, HALO):
+                    seen = key_row > query_col if c == 0 else key_row <= query_col
+                    part = jnp.where(seen, part, NEG)
+                    s_buf[c * ROWS : (c + 1) * ROWS] = part
+                highest = fold(jnp.maximum, part)
+                peak = jnp.maximum(peak, highest if c == HALO else jnp.where(inside[c], highest, NEG))
             peak = jnp.max(peak, axis=0, keepdims=True)
+            peaks = [jnp.where(inside[c], peak, -NEG) for c in range(HALO)] + [peak]
             total = jnp.zeros((8, ROWS), jnp.float32)
             centre = jnp.zeros((8, ROWS), jnp.float32)
             step = 64
             for begin in range(0, SPAN * ROWS, step):
                 at = slice(begin, begin + step)
-                raised = jnp.exp2((s_buf[at] - peak) * (SCALE * LOG2E))
+                raised = jnp.exp2((s_buf[at] - peaks[begin // ROWS]) * (SCALE * LOG2E))
                 s_buf[at] = raised
                 total = total + fold(jnp.add, raised)
                 centre = centre + fold(jnp.add, raised * g_buf[at])
@@ -236,19 +242,16 @@
             for begin in range(0, SPAN * ROWS, step):
                 at = slice(begin, begin + step)
                 prob = s_buf[at] * scale
-                p_low[at] = prob.astype(jnp.bfloat16)
-                s_low[at] = (prob * (g_buf[at] - centre)).astype(jnp.bfloat16)
-            nn = (((1,), (0,)), ((), ()))
-            key_part = lax.dot_general(s_low[...], query, nn, preferred_element_type=jnp.float32)
-            value_part = lax.dot_general(p_low[...], grad, nn, preferred_element_type=jnp.float32)
+                p_low[at, cols] = prob.astype(jnp.bfloat16)
+                s_low[at, cols] = (prob * (g_buf[at] - centre)).astype(jnp.bfloat16)
+            query_part = lax.dot_general(s_low[:, cols], keys, tn, preferred_element_type=jnp.float32)
+            dq_low[j, i, :, hh * HEAD_DIM : (hh + 1) * HEAD_DIM] = (query_part * SCALE).astype(jnp.bfloat16)
+        for low, first, out in ((s_low, 0, 0), (p_low, PAIR, HEAD_DIM)):
+            heads = [qg[j, i, :, first + hh * HEAD_DIM : first + (hh + 1) * HEAD_DIM] for hh in range(GROUP)]
+            both = jnp.concatenate(heads, axis=0)
+            whole = lax.dot_general(low[...], both, nn, preferred_element_type=jnp.float32)
             for c in range(SPAN):
-                at = slice(c * ROWS, (c + 1) * ROWS)
-                dkv[j, r + c, :, 0:HEAD_DIM] += key_part[at]
-                dkv[j, r + c, :, HEAD_DIM:] += value_part[at]
-            query_part = lax.dot_general(
-                s_low[...], keys, (((0,), (0,)), ((), ())), preferred_element_type=jnp.float32
-            )
-            dq_low[j, i, :, hh * HEAD_DIM : (hh + 1) * HEAD_DIM] = (query_part * SCALE).astype(jnp.bfloat16)
+                dkv[j, r + c, :, out : out + HEAD_DIM] += whole[c * ROWS : (c + 1) * ROWS]
 
     def rounded(j, b, extras=()):
         key_grad = dkv[j, b, :, 0:HEAD_DIM] * SCALE
@@ -279,7 +282,9 @@
         lax.fori_loop(0, HALO, one, 0)
 
     def give_twin(j):
-        got_blocks(back_in.at[j], back_recv.at[j], (core == 1) & (y == 0))
+        @pl.when(core == 0)
+        def _():
+            got(back_in.at[j], back_recv.at[j])
 
         def one(n, carry):
             i = lax.rem(x + jnp.where(n == 0, 2, jnp.where(n == 1, 1, jnp.where(n == 2, 3, 0))), ALONG)
@@ -319,6 +324,10 @@
                 give(dq_low.at[j, i, half], dq_hbm.at[half, pl.ds(col, PAIR)], 0, i)
 
     def give_kv(j):
+        @pl.when(core == 1)
+        def _():
+            got_blocks(back_in.at[j], back_recv.at[j], y == 0)
+
         col = pl.multiple_of((x * HEADS_KV + j) * HEAD_DIM, HEAD_DIM)
 
         def one(n, carry):
@@ -366,12 +375,11 @@
 
     def head(j, carry):
         got_blocks(kv.at[j], halo_recv.at[j], (core == 0) & (y == 1))
-        for i in range(ALONG):
-            got(qg.at[j, i], qg_sem.at[j, i])
-
         def half(part, carry):
             def one(n, carry):
-                unit(j, 2 * part + lax.rem(x + n, 2))
+                i = 2 * part + lax.rem(x + n, 2)
+                got(qg.at[j, i], qg_sem.at[j, i])
+                unit(j, i)
                 return carry
 
             lax.fori_loop(0, 2, one, 0)
@@ -391,8 +399,8 @@
             return carry
 
         lax.fori_loop(0, 2, half, 0)
+        give_twin(j)
         give_query(j)
-        give_twin(j)
 
         @pl.when(j >= 1)
         def _():
@@ -449,10 +457,10 @@
             pltpu.VMEM((HEADS_KV, HALO, ROWS, 2 * HEAD_DIM), jnp.bfloat16),
             pltpu.VMEM((HEADS_KV, ALONG, ROWS, 2 * HEAD_DIM), jnp.bfloat16),
             pltpu.VMEM((HEADS_KV, ALONG, ROWS, PAIR), jnp.bfloat16),
-            pltpu.VMEM((wide, ROWS), jnp.float32),
-            pltpu.VMEM((wide, ROWS), jnp.float32),
-            pltpu.VMEM((wide, ROWS), jnp.bfloat16),
-            pltpu.VMEM((wide, ROWS), jnp.bfloat16),
+            pltpu.VMEM((GROUP, wide, ROWS), jnp.float32),
+            pltpu.VMEM((GROUP, wide, ROWS), jnp.float32),
+            pltpu.VMEM((wide, GROUP * ROWS), jnp.bfloat16),
+            pltpu.VMEM((wide, GROUP * ROWS), jnp.bfloat16),
             dma((HEADS_KV, ALONG)),
             dma((HEADS_KV, ALONG)),
             dma((len(STEPS),)),

time: 128 us -> 125 us (0.977); the launches traced: 126 us -> 125 us
  no operation moved by 1% of the time
where the time goes in v5:
time: 125 us
  Pallas kernels  124 us (99%)
    pallas_call x1, Pallas kernels, local(): pl.pallas_call(functools.partial(kernel, lax.axis_size('seq')), out_shape...  122 us

profile of v5, /device:TPU:0, one launch (start us, length us, event | category | flops | bytes accessed | tf_op | source)
XLA Modules:
  0.0 124.9 jit_solution(14490560758567238724)
XLA Ops:
  0.6 122.2 %window_grads.1 = (bf16[256,4096]{1,0:T(8,128)(2,1)S(1)}, bf16[256,2048]{1,0:T(8,128)(2,1)S(1)}, bf16[256,2048]{1,0:T(8,128)(2,1)S(1)}) custom-call(bf16[256,4096]{1,0:T(8,128)(2,1)} %q_hbm.1, bf16[256,2048]{1,0:T(8,128)(2,1)} %k_hbm.1, bf16[256,2048]{1,0:T(8,128)(2,1)} %v_hbm.1, bf16[256,4096]{1,0:T(8,128)(2,1)} %g_hbm.1), custom_call_target="tpu_custom_call" | custom-call | tf_op jit(solution)/shard_map/window_grads/pallas_call | solution.py:447
  122.8 2.1 %write_out.1 = (bf16[256,4096]{1,0:T(8,128)(2,1)}, bf16[256,2048]{1,0:T(8,128)(2,1)}, bf16[256,2048]{1,0:T(8,128)(2,1)}) custom-call(bf16[256,4096]{1,0:T(8,128)(2,1)S(1)} %get-tuple-element.6.refs_0_, bf16[256,2048]{1,0:T(8,128)(2,1)S(1)} %get-tuple-element.7.refs_1_, bf16[256,2048]{1,0:T(8,128)(2,1)S(1)} %get-tuple-element.8.refs_2_), custom_call_target="tpu_custom_call" | custom-call | tf_op jit(solution)/shard_map/write_out/pallas_call | solution.py:479

commit v6 on v5

--- a/solution.py
+++ b/solution.py
@@ -376,13 +376,10 @@
     def head(j, carry):
         got_blocks(kv.at[j], halo_recv.at[j], (core == 0) & (y == 1))
         def half(part, carry):
-            def one(n, carry):
+            for n in range(2):
                 i = 2 * part + lax.rem(x + n, 2)
                 got(qg.at[j, i], qg_sem.at[j, i])
                 unit(j, i)
-                return carry
-
-            lax.fori_loop(0, 2, one, 0)
 
             @pl.when(part == 0)
             def _():

time: 125 us -> 125 us (level)
  no operation moved by 1% of the time
where the time goes in v6:
time: 125 us
  Pallas kernels  124 us (99%)
    pallas_call x1, Pallas kernels, local(): pl.pallas_call(functools.partial(kernel, lax.axis_size('seq')), out_shape...  122 us

profile of v6, /device:TPU:0, one launch (start us, length us, event | category | flops | bytes accessed | tf_op | source)
XLA Modules:
  0.0 124.9 jit_solution(16624047329163952083)
XLA Ops:
  0.6 122.2 %window_grads.1 = (bf16[256,4096]{1,0:T(8,128)(2,1)S(1)}, bf16[256,2048]{1,0:T(8,128)(2,1)S(1)}, bf16[256,2048]{1,0:T(8,128)(2,1)S(1)}) custom-call(bf16[256,4096]{1,0:T(8,128)(2,1)} %q_hbm.1, bf16[256,2048]{1,0:T(8,128)(2,1)} %k_hbm.1, bf16[256,2048]{1,0:T(8,128)(2,1)} %v_hbm.1, bf16[256,4096]{1,0:T(8,128)(2,1)} %g_hbm.1), custom_call_target="tpu_custom_call" | custom-call | tf_op jit(solution)/shard_map/window_grads/pallas_call | solution.py:444
  122.8 2.1 %write_out.1 = (bf16[256,4096]{1,0:T(8,128)(2,1)}, bf16[256,2048]{1,0:T(8,128)(2,1)}, bf16[256,2048]{1,0:T(8,128)(2,1)}) custom-call(bf16[256,4096]{1,0:T(8,128)(2,1)S(1)} %get-tuple-element.6.refs_0_, bf16[256,2048]{1,0:T(8,128)(2,1)S(1)} %get-tuple-element.7.refs_1_, bf16[256,2048]{1,0:T(8,128)(2,1)S(1)} %get-tuple-element.8.refs_2_), custom_call_target="tpu_custom_call" | custom-call | tf_op jit(solution)/shard_map/write_out/pallas_call | solution.py:476
